TPU v7x, 256 devices: a whole 4x4x8 slice. The times are simulated.
256 devices in a mesh: blk: 128 (over y, z, x_hi, core), dp: 2 (over x_lo).
Axes of the slice: x: 4 (x_hi: 2, x_lo: 2; x = x_hi * 2 + x_lo), y: 4, z: 8, core: 2. Of those that a mesh axis runs over, the one named last changes fastest.
Arguments:
- tokens: bfloat16 [32768, 3584], P(('blk', 'dp')), may hold values from -6 to 6
- route_dir: int32 [32768, 1], P(('blk', 'dp')), may hold values from 0 to 2; in each aligned block of 128 rows (0 to 127, 128 to 255, ...) at most 64 rows name the same one
- gate_probs: float32 [32768, 1], P(('blk', 'dp')), may hold values from 0.3 to 1
- gate_weight: bfloat16 [128, 3584, 512], P('blk', 'dp'), may hold values from -0.09375 to 0.09375
- up_weight: bfloat16 [128, 3584, 512], P('blk', 'dp'), may hold values from -0.09375 to 0.09375
- down_weight: bfloat16 [128, 3584, 512], P('blk', 'dp'), may hold values from -0.1875 to 0.1875
Outputs:
- d_tokens: bfloat16 [32768, 3584], P(('blk', 'dp'))
- grad_gate: bfloat16 [128, 3584, 512], P('blk', 'dp')
- grad_up: bfloat16 [128, 3584, 512], P('blk', 'dp')
- grad_down: bfloat16 [128, 3584, 512], P('blk', 'dp')
Inputs may be any that keep to these rules, and one draw needn't show every extreme that they name: A token on blk index b sends its row to expert e = (b // 2 + route_dir - 1) mod 64, whose halves sit at blk indices 2e and 2e + 1; on one device at most 64 tokens take the same value.
All inputs are finite; a program needn't handle non-finite values.
Results may differ from a plain program's by a relative error of at most 0.0079.
Values may be sent and summed in bfloat16 or wider, within the bound.
No kernel may reach another device: no remote copies, remote signals or barrier semaphores. Data moves between devices by JAX's collectives and lax.ppermute only.
A program may use at most 128 MiB of HBM per device.

v0:
```python
import jax
import jax.numpy as jnp
from jax import lax
from jax.sharding import PartitionSpec as P

CAP = 64


def shifted(shard, axis, by):
    length = lax.axis_size(axis)
    return lax.ppermute(shard, axis, [(i, (i + by) % length) for i in range(length)])


def partner_2(block, axis, bit):
    count = lax.axis_size(axis)
    route = []
    for low in range(count):
        high = low | 1 << bit
        if high != low and high < count:
            route += [(low, high), (high, low)]
    return lax.ppermute(block, axis, route)


def sent_together(arrays, axis, dim, along):
    both = jnp.concatenate(arrays, axis=along)
    filled, at, gathered = (lax.all_gather(both, axis, axis=dim, tiled=True), 0, [])
    for a in arrays:
        gathered.append(lax.slice_in_dim(filled, at, at + a.shape[along], axis=along))
        at += a.shape[along]
    return tuple(gathered)


def side_by_side(arrays, axis, dim, along):
    ends, at = ([], 0)
    for a in arrays[:-1]:
        at += a.shape[along]
        ends.append(at)
    both = jnp.concatenate(arrays, axis=along)
    return tuple(
        jnp.split(lax.psum_scatter(both, axis, scatter_dimension=dim, tiled=True), ends, axis=along)
    )


def selection(directions, capacity):
    slot_ids = jnp.arange(capacity, dtype=jnp.int32)
    planes = []
    for direction in range(3):
        chosen = (directions == direction).astype(jnp.int32)
        places = jnp.cumsum(chosen, axis=-1, dtype=jnp.int32) - 1
        matches = (chosen[..., None, :] == 1) & (places[..., None, :] == slot_ids[:, None])
        planes.append(matches)
    return jnp.stack(planes, axis=-3).astype(jnp.bfloat16)


def matmul(left_side, right_side):
    return jnp.dot(left_side, right_side, preferred_element_type=jnp.float32)


def times_transposed(left_side, right_side):
    return lax.dot_general(
        left_side, right_side, (((1,), (1,)), ((), ())), preferred_element_type=jnp.float32
    )


def transposed_times(left_side, right_side):
    return lax.dot_general(
        left_side, right_side, (((0,), (0,)), ((), ())), preferred_element_type=jnp.float32
    )


def activate(pre_gate, pre_up):
    sigmoid = jax.nn.sigmoid(pre_gate)
    return ((pre_gate * sigmoid * pre_up).astype(jnp.bfloat16), sigmoid)


def hidden_grads(d_hidden, pre_gate, pre_up, sigmoid):
    d_gate = (d_hidden * pre_up * (sigmoid * (1.0 + pre_gate * (1.0 - sigmoid)))).astype(
        jnp.bfloat16
    )
    d_up = (d_hidden * (pre_gate * sigmoid)).astype(jnp.bfloat16)
    return (d_gate, d_up)


def to_lower(payload):
    return shifted(payload, "blk", -2)


def to_upper(payload):
    return shifted(payload, "blk", 2)


def partner(payload):
    return partner_2(payload, "blk", 0)


def deliver(outgoing):
    own_rows = jnp.stack([to_lower(outgoing[0]), outgoing[1], to_upper(outgoing[2])])
    theirs = partner(own_rows)
    return jnp.concatenate([own_rows, theirs]).reshape(-1, own_rows.shape[-1])


def settle(partial_value):
    blocks = partial_value.reshape(6, -1, partial_value.shape[-1])
    received = partner(blocks[3:])
    own_part = lax.optimization_barrier(blocks[:3]).astype(jnp.float32)
    combined = (own_part + received.astype(jnp.float32)).astype(jnp.bfloat16)
    return jnp.stack([to_upper(combined[0]), combined[1], to_lower(combined[2])])


def unpack(selector, rows_back):
    return jnp.einsum("jst,jsd->td", selector, rows_back, preferred_element_type=jnp.float32)


def select_rows(selector, source_rows):
    return jnp.einsum(
        "jst,td->jsd", selector, source_rows, preferred_element_type=jnp.float32
    ).astype(jnp.bfloat16)


def per_device(tokens, route_dir, gate_probs, gate_weight, up_weight, down_weight):
    selector = selection(route_dir[:, 0], CAP)
    inputs = deliver(select_rows(selector, tokens))
    w_gate, w_up, w_down = sent_together((gate_weight[0], up_weight[0], down_weight[0]), "dp", 0, 1)
    pre_gate = matmul(inputs, w_gate)
    pre_up = matmul(inputs, w_up)
    activated, sigmoid = activate(pre_gate, pre_up)
    partial_value = times_transposed(activated, w_down).astype(jnp.bfloat16)
    result = gate_probs * unpack(selector, settle(partial_value))
    back_source = (gate_probs * result).astype(jnp.bfloat16)
    back_rows = deliver(select_rows(selector, back_source))
    d_hidden = matmul(back_rows, w_down)
    d_gate, d_up = hidden_grads(d_hidden, pre_gate, pre_up, sigmoid)
    summed_gate, summed_up, summed_down = tuple(
        (
            part.astype(jnp.float32)
            for part in side_by_side(
                (
                    transposed_times(inputs, d_gate).astype(jnp.bfloat16),
                    transposed_times(inputs, d_up).astype(jnp.bfloat16),
                    transposed_times(back_rows, activated).astype(jnp.bfloat16),
                ),
                "dp",
                0,
                1,
            )
        )
    )
    grad_gate = summed_gate.astype(jnp.bfloat16)[None]
    grad_up = summed_up.astype(jnp.bfloat16)[None]
    grad_down = summed_down.astype(jnp.bfloat16)[None]
    dx_part = (times_transposed(d_gate, w_gate) + times_transposed(d_up, w_up)).astype(jnp.bfloat16)
    d_tokens = unpack(selector, settle(dx_part)).astype(jnp.bfloat16)
    return (d_tokens, grad_gate, grad_up, grad_down)


def solution(mesh):
    return jax.shard_map(
        per_device,
        mesh=mesh,
        in_specs=(
            P(("blk", "dp"), None),
            P(("blk", "dp"), None),
            P(("blk", "dp"), None),
            P("blk", "dp", None),
            P("blk", "dp", None),
            P("blk", "dp", None),
        ),
        out_specs=(
            P(("blk", "dp"), None),
            P("blk", "dp", None),
            P("blk", "dp", None),
            P("blk", "dp", None),
        ),
        check_vma=False,
    )
```

profile of v0, /device:TPU:1, one launch (start us, length us, event | category | flops | bytes accessed | tf_op | source)
XLA Modules:
  0.0 430.9 jit_solution(11241998296531300472)
XLA Ops:
  7.2 5.9 %pad_maximum_fusion.1 = bf16[1792,1536]{1,0:T(8,128)(2,1)} fusion(bf16[1792,512]{1,0:T(8,128)(2,1)} %bitcast.89, bf16[1792,512]{1,0:T(8,128)(2,1)} %bitcast.90, bf16[1792,512]{1,0:T(8,128)(2,1)} %bitcast.91), kind=kLoop, calls=%fused_computation.7 | loop fusion | flops 16515072 | bytes 11010048 | tf_op jit(solution)/shard_map/concatenate | solution.py:25
  13.1 0.0 reduce-scatter.2.cloned.1.call-start
  13.2 0.6 copy-done.4
  13.8 0.1 copy.18
  13.9 0.1 copy.16
  14.0 0.2 reduce-window.26
  14.2 0.2 reduce-window.24
  14.4 0.1 copy.17
  14.5 0.2 reduce-window.25
  14.6 0.1 add_reduce_fusion
  14.7 0.1 add_reduce_fusion.2
  14.9 0.1 add_reduce_fusion.1
  15.0 0.5 convolution_convert_fusion.5
  15.5 0.1 slice_bitcast_fusion.10
  15.6 3.7 collective-permute-start.1
  19.3 7.8 %collective-permute-start = (bf16[64,3584]{1,0:T(8,128)(2,1)S(1)}, bf16[64,3584]{1,0:T(8,128)(2,1)S(1)}, u32[]{:S(2)}, u32[]{:S(2)}) collective-permute-start(bf16[64,3584]{1,0:T(8,128)(2,1)S(1)} %get-tuple-element.30), channel_id=1, source_target_pairs={{0,252},{2,254},{4,0},{6,2},{8,4},{10,6},{12,8},{14,10},{16,12},{1... | collective-permute-start | bytes 1376264 | tf_op jit(solution)/shard_map/ppermute | solution.py:11
  27.1 11.9 %collective-permute-done.1 = bf16[64,3584]{1,0:T(8,128)(2,1)S(1)} collective-permute-done((bf16[64,3584]{1,0:T(8,128)(2,1)S(1)}, bf16[64,3584]{1,0:T(8,128)(2,1)S(1)}, u32[]{:S(2)}, u32[]{:S(2)}) %collective-permute-start.1) | collective-permute-done | bytes 458784 | tf_op jit(solution)/shard_map/ppermute | solution.py:11
  39.0 3.2 collective-permute-done
  42.3 0.2 pad_maximum_fusion.4
  42.4 4.9 %collective-permute-start.2 = (bf16[3,64,3584]{2,1,0:T(8,128)(2,1)S(1)}, bf16[3,64,3584]{2,1,0:T(8,128)(2,1)S(1)}, u32[]{:S(2)}, u32[]{:S(2)}) collective-permute-start(bf16[3,64,3584]{2,1,0:T(8,128)(2,1)S(1)} %pad_maximum_fusion.4), channel_id=1, source_target_pairs={{0,2},{2,0},{4,6},{6,4},{8,10},{10,8},{12,14},{14,12},{16,18},{18,... | collective-permute-start | bytes 4128776 | tf_op jit(solution)/shard_map/ppermute | solution.py:21
  47.3 2.8 collective-permute-done.2
  50.1 1.7 pad_maximum_fusion.2
  51.8 106.9 %all-gather.2.cloned.1.call-done = bf16[3584,1536]{1,0:T(8,128)(2,1)} async-done(((bf16[1792,1536]{1,0:T(8,128)(2,1)}), bf16[3584,1536]{1,0:T(8,128)(2,1)}) %all-gather.2.cloned.1.call-update) | async-done | bytes 11010064 | tf_op jit(solution)/shard_map/all_gather | solution.py:26
  158.7 4.6 %fusion.14 = f32[384,512]{1,0:T(8,128)S(1)} fusion(bf16[384,3584]{1,0:T(8,128)(2,1)} %bitcast.83, bf16[3584,1536]{1,0:T(8,128)(2,1)} %all-gather.2.cloned.1.call-done), kind=kOutput, calls=%fused_computation.25 | convolution fusion | flops 1409286144 | bytes 7208960 | tf_op jit(solution)/shard_map/dot_general | solution.py:56
  163.3 4.8 %multiply_convert_fusion.2 = (bf16[384,512]{1,0:T(8,128)(2,1)S(1)}, f32[384,512]{1,0:T(8,128)}) fusion(f32[384,512]{1,0:T(8,128)S(1)} %fusion.14, bf16[384,3584]{1,0:T(8,128)(2,1)S(1)} %bitcast.84, bf16[3584,1536]{1,0:T(8,128)(2,1)} %all-gather.2.cloned.1.call-done), kind=kOutput, calls=%fused_computation.50 | convolution fusion | flops 1410465792 | bytes 8388608 | tf_op jit(solution)/shard_map/dot_general | solution.py:56
  168.1 3.8 convolution_convert_fusion.3
  171.9 0.2 fusion.38
  172.1 0.5 collective-permute-start.3
  172.7 2.8 collective-permute-done.3
  175.4 0.3 add_convert_fusion.1
  175.7 0.1 slice_bitcast_fusion.8
  175.8 10.4 %collective-permute-start.5 = (bf16[64,3584]{1,0:T(8,128)(2,1)S(1)}, bf16[64,3584]{1,0:T(8,128)(2,1)S(1)}, u32[]{:S(2)}, u32[]{:S(2)}) collective-permute-start(bf16[64,3584]{1,0:T(8,128)(2,1)S(1)} %get-tuple-element.28), channel_id=1, source_target_pairs={{0,252},{2,254},{4,0},{6,2},{8,4},{10,6},{12,8},{14,10},{16,12},{1... | collective-permute-start | bytes 1376264 | tf_op jit(solution)/shard_map/ppermute | solution.py:11
  186.3 9.6 %collective-permute-done.5 = bf16[64,3584]{1,0:T(8,128)(2,1)S(1)} collective-permute-done((bf16[64,3584]{1,0:T(8,128)(2,1)S(1)}, bf16[64,3584]{1,0:T(8,128)(2,1)S(1)}, u32[]{:S(2)}, u32[]{:S(2)}) %collective-permute-start.5) | collective-permute-done | bytes 458784 | tf_op jit(solution)/shard_map/ppermute | solution.py:11
  195.9 7.6 %collective-permute-done.4 = bf16[64,3584]{1,0:T(8,128)(2,1)S(1)} collective-permute-done((bf16[64,3584]{1,0:T(8,128)(2,1)S(1)}, bf16[64,3584]{1,0:T(8,128)(2,1)S(1)}, u32[]{:S(2)}, u32[]{:S(2)}) %collective-permute-start.4) | collective-permute-done | bytes 458784 | tf_op jit(solution)/shard_map/ppermute | solution.py:11
  203.4 0.8 convolution_convert_fusion.4
  204.2 0.1 slice_bitcast_fusion.6
  204.3 0.8 collective-permute-start.7
  205.2 6.4 %collective-permute-start.6 = (bf16[64,3584]{1,0:T(8,128)(2,1)S(1)}, bf16[64,3584]{1,0:T(8,128)(2,1)S(1)}, u32[]{:S(2)}, u32[]{:S(2)}) collective-permute-start(bf16[64,3584]{1,0:T(8,128)(2,1)S(1)} %get-tuple-element.24), channel_id=1, source_target_pairs={{0,252},{2,254},{4,0},{6,2},{8,4},{10,6},{12,8},{14,10},{16,12},{1... | collective-permute-start | bytes 1376264 | tf_op jit(solution)/shard_map/ppermute | solution.py:11
  211.6 12.8 %collective-permute-done.7 = bf16[64,3584]{1,0:T(8,128)(2,1)S(1)} collective-permute-done((bf16[64,3584]{1,0:T(8,128)(2,1)S(1)}, bf16[64,3584]{1,0:T(8,128)(2,1)S(1)}, u32[]{:S(2)}, u32[]{:S(2)}) %collective-permute-start.7) | collective-permute-done | bytes 458784 | tf_op jit(solution)/shard_map/ppermute | solution.py:11
  224.4 4.5 %collective-permute-done.6 = bf16[64,3584]{1,0:T(8,128)(2,1)S(1)} collective-permute-done((bf16[64,3584]{1,0:T(8,128)(2,1)S(1)}, bf16[64,3584]{1,0:T(8,128)(2,1)S(1)}, u32[]{:S(2)}, u32[]{:S(2)}) %collective-permute-start.6) | collective-permute-done | bytes 458784 | tf_op jit(solution)/shard_map/ppermute | solution.py:11
  229.0 0.2 pad_maximum_fusion.5
  229.1 0.8 collective-permute-start.8
  229.9 2.8 collective-permute-done.8
  232.6 0.3 pad_maximum_fusion.3
  233.0 2.1 convolution_convert_fusion
  235.2 4.0 multiply_convert_fusion
  239.2 2.2 convolution_convert_fusion.1
  241.4 2.2 convolution_convert_fusion.2
  243.5 14.7 %pad_maximum_fusion = bf16[3584,1536]{0,1:T(8,128)(2,1)} fusion(bf16[3584,512]{0,1:T(8,128)(2,1)S(1)} %convolution_convert_fusion, bf16[3584,512]{0,1:T(8,128)(2,1)S(1)} %convolution_convert_fusion.1, bf16[3584,512]{0,1:T(8,128)(2,1)S(1)} %convolution_convert_fusion.2), kind=kLoop, calls=%fused_computation | loop fusion | flops 33030144 | bytes 22020096 | tf_op jit(solution)/shard_map/concatenate | solution.py:38
  258.2 3.7 fusion.12
  261.9 3.7 fusion
  265.5 0.2 fusion.37
  265.7 0.7 collective-permute-start.9
  266.4 2.8 collective-permute-done.9
  269.2 0.3 add_convert_fusion
  269.5 0.1 slice_bitcast_fusion.4
  269.6 5.5 %collective-permute-start.11 = (bf16[64,3584]{1,0:T(8,128)(2,1)S(1)}, bf16[64,3584]{1,0:T(8,128)(2,1)S(1)}, u32[]{:S(2)}, u32[]{:S(2)}) collective-permute-start(bf16[64,3584]{1,0:T(8,128)(2,1)S(1)} %get-tuple-element.22), channel_id=1, source_target_pairs={{0,252},{2,254},{4,0},{6,2},{8,4},{10,6},{12,8},{14,10},{16,12},{1... | collective-permute-start | bytes 1376264 | tf_op jit(solution)/shard_map/ppermute | solution.py:11
  275.1 28.0 %collective-permute-done.11 = bf16[64,3584]{1,0:T(8,128)(2,1)S(1)} collective-permute-done((bf16[64,3584]{1,0:T(8,128)(2,1)S(1)}, bf16[64,3584]{1,0:T(8,128)(2,1)S(1)}, u32[]{:S(2)}, u32[]{:S(2)}) %collective-permute-start.11) | collective-permute-done | bytes 458784 | tf_op jit(solution)/shard_map/ppermute | solution.py:11
  303.1 1.4 fusion.4
  304.4 104.8 %reduce-scatter.2.cloned.1.call-done = bf16[1792,1536]{0,1:T(8,128)(2,1)} async-done(((bf16[3584,1536]{0,1:T(8,128)(2,1)}), bf16[1792,1536]{0,1:T(8,128)(2,1)}) %reduce-scatter.2.cloned.1.call-update) | async-done | bytes 5505040 | tf_op jit(solution)/shard_map/reduce_scatter | solution.py:40
  409.3 4.8 %slice_bitcast_fusion = (bf16[1,1792,512]{1,2,0:T(8,128)(2,1)S(1)}, bf16[1,1792,512]{1,2,0:T(8,128)(2,1)}, bf16[1,1792,512]{1,2,0:T(8,128)(2,1)}) fusion(bf16[1792,1536]{0,1:T(8,128)(2,1)} %reduce-scatter.2.cloned.1.call-done), kind=kLoop, calls=%fused_computation.31 | loop fusion | bytes 11010048 | tf_op jit(solution)/shard_map/broadcast_in_dim | solution.py:150
  414.1 3.8 copy.19
  417.9 3.9 copy.20
  421.8 2.3 copy.21
  (30 shorter events, 0.2 us)
Async XLA Ops:
  7.2 7.9 %copy-start = (bf16[128,3584]{1,0:T(8,128)(2,1)S(1)}, bf16[128,3584]{1,0:T(8,128)(2,1)}, u32[]{:S(2)}) copy-start(bf16[128,3584]{1,0:T(8,128)(2,1)} %param.6) | copy-start | bytes 2752516
  7.2 151.5 %all-gather.2.cloned.1.call-start = ((), (), s32[]{:S(2)}) async-start(), calls=%async_computation.1 | async-start | bytes 16515072 | tf_op jit(solution)/shard_map/all_gather | solution.py:26
  13.1 0.7 copy-start.4
  13.1 396.1 %reduce-scatter.2.cloned.1.call-start = ((), (), s32[]{:S(2)}) async-start(), calls=%async_computation.2 | async-start | bytes 16515072 | tf_op jit(solution)/shard_map/reduce_scatter | solution.py:40
  15.6 23.4 %collective-permute-start.1 = (bf16[64,3584]{1,0:T(8,128)(2,1)S(1)}, bf16[64,3584]{1,0:T(8,128)(2,1)S(1)}, u32[]{:S(2)}, u32[]{:S(2)}) collective-permute-start(bf16[64,3584]{1,0:T(8,128)(2,1)S(1)} %get-tuple-element.31), channel_id=1, source_target_pairs={{0,4},{2,6},{4,8},{6,10},{8,12},{10,14},{12,16},{14,18},{16,20},{1... | collective-permute-start | bytes 1376264 | tf_op jit(solution)/shard_map/ppermute | solution.py:11
  19.3 23.0 %collective-permute-start = (bf16[64,3584]{1,0:T(8,128)(2,1)S(1)}, bf16[64,3584]{1,0:T(8,128)(2,1)S(1)}, u32[]{:S(2)}, u32[]{:S(2)}) collective-permute-start(bf16[64,3584]{1,0:T(8,128)(2,1)S(1)} %get-tuple-element.30), channel_id=1, source_target_pairs={{0,252},{2,254},{4,0},{6,2},{8,4},{10,6},{12,8},{14,10},{16,12},{1... | collective-permute-start | bytes 1376264 | tf_op jit(solution)/shard_map/ppermute | solution.py:11
  42.4 7.6 %collective-permute-start.2 = (bf16[3,64,3584]{2,1,0:T(8,128)(2,1)S(1)}, bf16[3,64,3584]{2,1,0:T(8,128)(2,1)S(1)}, u32[]{:S(2)}, u32[]{:S(2)}) collective-permute-start(bf16[3,64,3584]{2,1,0:T(8,128)(2,1)S(1)} %pad_maximum_fusion.4), channel_id=1, source_target_pairs={{0,2},{2,0},{4,6},{6,4},{8,10},{10,8},{12,14},{14,12},{16,18},{18,... | collective-permute-start | bytes 4128776 | tf_op jit(solution)/shard_map/ppermute | solution.py:21
  158.7 4.6 %copy-start.2 = (bf16[6,64,3584]{2,1,0:T(8,128)(2,1)S(1)}, bf16[6,64,3584]{2,1,0:T(8,128)(2,1)}, u32[]{:S(2)}) copy-start(bf16[6,64,3584]{2,1,0:T(8,128)(2,1)} %pad_maximum_fusion.2) | copy-start | bytes 8257540
  163.3 4.8 %copy-start.8 = (f32[384,512]{1,0:T(8,128)}, f32[384,512]{1,0:T(8,128)S(1)}, u32[]{:S(2)}) copy-start(f32[384,512]{1,0:T(8,128)S(1)} %fusion.14) | copy-start | bytes 2359300
  168.1 3.8 copy-start.6
  172.1 3.3 collective-permute-start.3
  172.7 30.8 %copy-start.5 = (f32[128,1]{0,1:T(1,128)S(1)}, f32[128,1]{0,1:T(1,128)}, u32[]{:S(2)}) copy-start(f32[128,1]{0,1:T(1,128)} %param.8) | copy-start | bytes 1540
  175.8 20.0 %collective-permute-start.5 = (bf16[64,3584]{1,0:T(8,128)(2,1)S(1)}, bf16[64,3584]{1,0:T(8,128)(2,1)S(1)}, u32[]{:S(2)}, u32[]{:S(2)}) collective-permute-start(bf16[64,3584]{1,0:T(8,128)(2,1)S(1)} %get-tuple-element.28), channel_id=1, source_target_pairs={{0,252},{2,254},{4,0},{6,2},{8,4},{10,6},{12,8},{14,10},{16,12},{1... | collective-permute-start | bytes 1376264 | tf_op jit(solution)/shard_map/ppermute | solution.py:11
  186.3 17.1 %collective-permute-start.4 = (bf16[64,3584]{1,0:T(8,128)(2,1)S(1)}, bf16[64,3584]{1,0:T(8,128)(2,1)S(1)}, u32[]{:S(2)}, u32[]{:S(2)}) collective-permute-start(bf16[64,3584]{1,0:T(8,128)(2,1)S(1)} %get-tuple-element.27), channel_id=1, source_target_pairs={{0,4},{2,6},{4,8},{6,10},{8,12},{10,14},{12,16},{14,18},{16,20},{1... | collective-permute-start | bytes 1376264 | tf_op jit(solution)/shard_map/ppermute | solution.py:11
  204.3 20.1 %collective-permute-start.7 = (bf16[64,3584]{1,0:T(8,128)(2,1)S(1)}, bf16[64,3584]{1,0:T(8,128)(2,1)S(1)}, u32[]{:S(2)}, u32[]{:S(2)}) collective-permute-start(bf16[64,3584]{1,0:T(8,128)(2,1)S(1)} %get-tuple-element.25), channel_id=1, source_target_pairs={{0,4},{2,6},{4,8},{6,10},{8,12},{10,14},{12,16},{14,18},{16,20},{1... | collective-permute-start | bytes 1376264 | tf_op jit(solution)/shard_map/ppermute | solution.py:11
  205.2 23.8 %collective-permute-start.6 = (bf16[64,3584]{1,0:T(8,128)(2,1)S(1)}, bf16[64,3584]{1,0:T(8,128)(2,1)S(1)}, u32[]{:S(2)}, u32[]{:S(2)}) collective-permute-start(bf16[64,3584]{1,0:T(8,128)(2,1)S(1)} %get-tuple-element.24), channel_id=1, source_target_pairs={{0,252},{2,254},{4,0},{6,2},{8,4},{10,6},{12,8},{14,10},{16,12},{1... | collective-permute-start | bytes 1376264 | tf_op jit(solution)/shard_map/ppermute | solution.py:11
  229.1 3.9 copy-start.7
  229.1 3.5 collective-permute-start.8
  233.0 2.2 copy-start.9
  233.0 2.2 copy-start.10
  235.2 4.0 copy-start.3
  265.7 3.4 collective-permute-start.9
  269.6 33.5 %collective-permute-start.11 = (bf16[64,3584]{1,0:T(8,128)(2,1)S(1)}, bf16[64,3584]{1,0:T(8,128)(2,1)S(1)}, u32[]{:S(2)}, u32[]{:S(2)}) collective-permute-start(bf16[64,3584]{1,0:T(8,128)(2,1)S(1)} %get-tuple-element.22), channel_id=1, source_target_pairs={{0,252},{2,254},{4,0},{6,2},{8,4},{10,6},{12,8},{14,10},{16,12},{1... | collective-permute-start | bytes 1376264 | tf_op jit(solution)/shard_map/ppermute | solution.py:11
  275.1 28.0 %collective-permute-start.10 = (bf16[64,3584]{1,0:T(8,128)(2,1)S(1)}, bf16[64,3584]{1,0:T(8,128)(2,1)S(1)}, u32[]{:S(2)}, u32[]{:S(2)}) collective-permute-start(bf16[64,3584]{1,0:T(8,128)(2,1)S(1)} %get-tuple-element.21), channel_id=1, source_target_pairs={{0,4},{2,6},{4,8},{6,10},{8,12},{10,14},{12,16},{14,18},{16,20},{1... | collective-permute-start | bytes 1376264 | tf_op jit(solution)/shard_map/ppermute | solution.py:11
  417.9 6.2 %copy-start.1 = (bf16[128,3584]{1,0:T(8,128)(2,1)S(1)}, bf16[128,3584]{1,0:T(8,128)(2,1)}, u32[]{:S(2)}) copy-start(bf16[128,3584]{1,0:T(8,128)(2,1)} %param.6) | copy-start | bytes 2752516
Sparse Core Ops, SparseCore 0:
  13.3 145.3 all-gather.1
  258.3 150.8 reduce-scatter.1
where the time goes:
time: 431 us
  waiting for transfers between devices  300 us (70%)
  starting transfers between devices  41.7 us (10%)
  matrix products  33.7 us (8%)
  other arithmetic  24.4 us (6%)
  local copies, waits for them, and re-layouts  16.5 us (4%)
  between operations  14.3 us (3%)
    all_gather x1, waiting for transfers between devices, sent_together(): lax.all_gather(both, axis, axis=dim, tiled=True)  107 us
    reduce_scatter x1, waiting for transfers between devices, side_by_side(): lax.psum_scatter(both, axis, scatter_dimension=dim, tiled=True)  105 us
    ppermute x8, waiting for transfers between devices, shifted(): lax.ppermute(shard, axis, [(i, (i + by) % length) for i in range(length)])  77.6 us
    ppermute x8, starting transfers between devices, shifted(): lax.ppermute(shard, axis, [(i, (i + by) % length) for i in range(length)])  34.7 us
    concatenate x1, other arithmetic, side_by_side(): both = jnp.concatenate(arrays, axis=along)  14.7 us
    dot_general x3, matrix products, matmul(): return jnp.dot(left_side, right_side, preferred_element_type=jnp.float32)  13.4 us
    dot_general x3, matrix products, times_transposed(): lax.dot_general(left_side, right_side, (((1,), (1,)), ((), ())), preferre...  11.1 us
    ppermute x4, waiting for transfers between devices, partner_2(): return lax.ppermute(block, axis, route)  11 us
  transfers between devices with their start and end apart: 14, of which 13 were waited for; matrix products, arithmetic and copies ran while one was open for 3% of the time, Pallas kernels for 0%

commit v1 on v0

v1 whole, which is shorter than its diff:
```python
import functools

import jax
import jax.numpy as jnp
from jax import lax
from jax.experimental import pallas as pl
from jax.experimental.pallas import tpu as pltpu
from jax.sharding import PartitionSpec as P

CAP = 64
EXTRA = 128
BF16 = jnp.bfloat16
F32 = jnp.float32
PARAMS = pltpu.CompilerParams(vmem_limit_bytes=20 * 1024 * 1024)
SMALL = pltpu.CompilerParams(vmem_limit_bytes=12 * 1024 * 1024)


def dot(a, b):
    return lax.dot_general(a, b, (((1,), (0,)), ((), ())), preferred_element_type=F32)


def dot_t(a, b):
    return lax.dot_general(a, b, (((1,), (1,)), ((), ())), preferred_element_type=F32)


def t_dot(a, b):
    return lax.dot_general(a, b, (((0,), (0,)), ((), ())), preferred_element_type=F32)


def send(x, by, flip, tag):
    n, m = lax.axis_size("blk"), lax.axis_size("dp")
    route = [(b * m + d, ((b + by) % n) * m + (d ^ flip)) for b in range(n) for d in range(m)]
    with jax.named_scope(tag):
        return lax.ppermute(x, ("blk", "dp"), route)


def swap_dp(x, tag):
    with jax.named_scope(tag):
        return lax.ppermute(x, "dp", [(0, 1), (1, 0)])


def swap_core(x, tag):
    with jax.named_scope(tag):
        return lax.ppermute(x, "blk", [(i, i ^ 1) for i in range(lax.axis_size("blk"))])


def after(x, *earlier):
    return lax.optimization_barrier((x,) + earlier)[0]


def select_kernel(d_ref, tokens, route, gate, sel_ref, *outs):
    count, width = tokens.shape
    half = width // 2
    d = d_ref[0]
    row = lax.broadcasted_iota(jnp.int32, (count, count), 0)
    col = lax.broadcasted_iota(jnp.int32, (count, count), 1)
    upper = jnp.where(row <= col, 1.0, 0.0).astype(BF16)
    chosen = jnp.where(route[...] == row, 1.0, 0.0)
    counts = dot(chosen.astype(BF16), upper)
    slot = lax.broadcasted_iota(jnp.int32, (CAP, count), 0).astype(F32)
    lane = lax.broadcasted_iota(jnp.int32, (CAP, EXTRA), 1)
    for j in range(3):
        hit = (chosen[j : j + 1, :] > 0.5) & (counts[j : j + 1, :] - 1.0 == slot)
        value = jnp.sum(jnp.where(hit, gate[...], 0.0), axis=1, keepdims=True)
        high = value.astype(BF16).astype(F32)
        picked = jnp.where(lane == 0, high, jnp.where(lane == 1, value - high, 0.0)).astype(BF16)
        sel = jnp.where(hit, 1.0, 0.0).astype(BF16)
        sel_ref[j * CAP : (j + 1) * CAP, :] = sel
        for k, which in enumerate((d, 1 - d)):
            at = pl.multiple_of(which * half, 128)
            outs[2 * j + k][:, :half] = dot(sel, tokens[:, pl.ds(at, half)]).astype(BF16)
            outs[2 * j + k][:, half:] = picked


def select(d, tokens, route_dir, gate_probs):
    count, width = tokens.shape
    piece = jax.ShapeDtypeStruct((CAP, width // 2 + EXTRA), BF16)
    vmem = pl.BlockSpec(memory_space=pltpu.VMEM)
    return pl.pallas_call(
        select_kernel,
        out_shape=(jax.ShapeDtypeStruct((3 * CAP, count), BF16),) + (piece,) * 6,
        in_specs=[pl.BlockSpec(memory_space=pltpu.SMEM), vmem, vmem, vmem],
        out_specs=(vmem,) * 7,
        compiler_params=PARAMS,
        name="select",
    )(d, tokens, route_dir.reshape(1, count), gate_probs.reshape(1, count))


def reorder(x):
    return jnp.concatenate([x[CAP * i : CAP * (i + 1)] for i in (1, 0, 3, 2)], axis=0)


def both(sent, got):
    return reorder(sent[...]).astype(F32) + got[...].astype(F32)


def pre_kernel(a, b, c, d, wg, wu, x_out, gates, out):
    width, f = wg.shape
    pieces = (a, b, c, d)
    x = jnp.concatenate([p[:, :width] for p in pieces], axis=0)
    x_out[...] = x
    gates[...] = jnp.concatenate([p[:, width:] for p in pieces], axis=0)
    for k, w in enumerate((wg, wu)):
        out[:, k * f : (k + 1) * f] = reorder(dot(x, w[...]).astype(BF16))


def pre(pieces, wg, wu):
    rows, (width, f) = 4 * CAP, wg.shape
    return pl.pallas_call(
        pre_kernel,
        out_shape=(
            jax.ShapeDtypeStruct((rows, width), BF16),
            jax.ShapeDtypeStruct((rows, EXTRA), BF16),
            jax.ShapeDtypeStruct((rows, 2 * f), BF16),
        ),
        compiler_params=SMALL,
        name="pre",
    )(*pieces, wg, wu)


def down_kernel(sent, got, wd, hidden, part):
    f = wd.shape[1]
    value = both(sent, got)
    pg, pu = value[:, :f], value[:, f:]
    h = (pg * jax.nn.sigmoid(pg) * pu).astype(BF16)
    hidden[...] = h
    value = dot_t(h, wd[...]).astype(BF16)
    rows = value.shape[0] // 2
    part[:rows] = value[rows:]
    part[rows:] = value[:rows]


def down(sent, got, wd):
    rows = sent.shape[0]
    width, f = wd.shape
    return pl.pallas_call(
        down_kernel,
        out_shape=(
            jax.ShapeDtypeStruct((rows, f), BF16),
            jax.ShapeDtypeStruct((rows, width), BF16),
        ),
        compiler_params=SMALL,
        name="down",
    )(sent, got, wd)


def turn_kernel(part, got, gates, wd, back_out, dh):
    rows = part.shape[0] // 2
    own = jnp.concatenate([part[rows:], part[:rows]], axis=0)
    expert_out = own.astype(F32) + got[...].astype(F32)
    gate = gates[:, 0:1].astype(F32) + gates[:, 1:2].astype(F32)
    back = (gate * (gate * expert_out)).astype(BF16)
    back_out[...] = back
    dh[...] = reorder(dot(back, wd[...]).astype(BF16))


def turn(part, got, gates, wd):
    rows = part.shape[0]
    width, f = wd.shape
    return pl.pallas_call(
        turn_kernel,
        out_shape=(
            jax.ShapeDtypeStruct((rows, width), BF16),
            jax.ShapeDtypeStruct((rows, f), BF16),
        ),
        compiler_params=SMALL,
        name="turn",
    )(part, got, gates, wd)


def back_kernel(sent, got, dh_sent, dh_got, wg, wu, acts, own, part):
    f = wg.shape[1]
    value = both(sent, got)
    pg, pu = value[:, :f], value[:, f:]
    dh = both(dh_sent, dh_got)
    s = jax.nn.sigmoid(pg)
    dg = (dh * pu * (s * (1.0 + pg * (1.0 - s)))).astype(BF16)
    du = (dh * (pg * s)).astype(BF16)
    acts[:, :f] = dg
    acts[:, f:] = du
    value = (dot_t(dg, wg[...]) + dot_t(du, wu[...])).astype(BF16)
    rows = value.shape[0] // 2
    own[...] = value[:rows]
    part[...] = value[rows:]


def back(sent, got, dh_sent, dh_got, wg, wu):
    rows = sent.shape[0]
    width, f = wg.shape
    half = jax.ShapeDtypeStruct((rows // 2, width), BF16)
    return pl.pallas_call(
        back_kernel,
        out_shape=(jax.ShapeDtypeStruct((rows, 2 * f), BF16), half, half),
        compiler_params=SMALL,
        name="back",
    )(sent, got, dh_sent, dh_got, wg, wu)


def add_kernel(own, got, same, other):
    value = (own[...].astype(F32) + got[...].astype(F32)).astype(BF16)
    same[...] = value[:CAP]
    other[...] = value[CAP:]


def add(own, got):
    piece = jax.ShapeDtypeStruct((CAP, own.shape[1]), BF16)
    return pl.pallas_call(
        add_kernel, out_shape=(piece, piece), compiler_params=SMALL, name="add"
    )(own, got)


def unpack_kernel(d_ref, sel, s0, s1, s2, o0, o1, o2, out):
    half = s0.shape[1]
    d = d_ref[0]
    for which, parts in ((d, (s0, s1, s2)), (1 - d, (o0, o1, o2))):
        at = pl.multiple_of(which * half, 128)
        rows = jnp.concatenate([p[...] for p in parts], axis=0)
        out[:, pl.ds(at, half)] = t_dot(sel[...], rows).astype(BF16)


def unpack(d, sel, same, other):
    count, half = sel.shape[1], same[0].shape[1]
    vmem = pl.BlockSpec(memory_space=pltpu.VMEM)
    return pl.pallas_call(
        unpack_kernel,
        out_shape=jax.ShapeDtypeStruct((count, 2 * half), BF16),
        in_specs=[pl.BlockSpec(memory_space=pltpu.SMEM)] + [vmem] * 7,
        out_specs=vmem,
        compiler_params=PARAMS,
        name="unpack",
    )(d, sel, *same, *other)


def grads_kernel(counts, *refs):
    groups = []
    for n in counts:
        groups.append(jnp.concatenate([r[...] for r in refs[:n]], axis=0))
        refs = refs[n:]
    x, acts, back_rows, hidden = groups
    gate_out, up_out, down_out = refs
    f = hidden.shape[1]
    up = t_dot(x, acts).astype(BF16)
    gate_out[...] = up[:, :f]
    up_out[...] = up[:, f:]
    down_out[...] = t_dot(back_rows, hidden).astype(BF16)


def grads(xs, acts, backs, hidden):
    width, f, tile = backs[0].shape[1], hidden[0].shape[1], 256

    def whole(x):
        return pl.BlockSpec(x.shape, lambda i: (0, 0))

    def columns(x):
        return pl.BlockSpec((x.shape[0], tile), lambda i: (0, i))

    out = pl.BlockSpec((tile, f), lambda i: (i, 0))
    return pl.pallas_call(
        functools.partial(grads_kernel, (len(xs), len(acts), len(backs), len(hidden))),
        grid=(width // tile,),
        in_specs=[columns(x) for x in xs]
        + [whole(x) for x in acts]
        + [columns(x) for x in backs]
        + [whole(x) for x in hidden],
        out_specs=[out] * 3,
        out_shape=[jax.ShapeDtypeStruct((width, f), BF16)] * 3,
        compiler_params=PARAMS,
        name="grads",
    )(*xs, *acts, *backs, *hidden)


def per_device(tokens, route_dir, gate_probs, gate_weight, up_weight, down_weight):
    d = lax.axis_index("dp").astype(jnp.int32).reshape(1)
    yes = d[0] < 2
    wg, wu, wd = gate_weight[0], up_weight[0], down_weight[0]

    def together(f, *args):
        shapes = jax.eval_shape(f, *args)

        def zeros(*_):
            return jax.tree.map(lambda s: jnp.zeros(s.shape, s.dtype), shapes)

        return lax.cond(yes, f, zeros, *args)

    def first(xs, xo, wg, wu):
        return pre((xs, xo, swap_core(xs, "cs"), swap_core(xo, "cx")), wg, wu)

    def middle(sent, got, gates, wd):
        h, part = down(sent, got, wd)
        return h, *turn(part, swap_core(part, "eo"), gates, wd)

    def last(sent, got, dh, dg, wg, wu):
        acts, own, part = back(sent, got, dh, dg, wg, wu)
        return acts, *add(own, swap_core(part, "dx"))

    sel, p_s, p_o, o_s, o_o, n_s, n_o = select(d, tokens, route_dir, gate_probs)
    o_x = swap_dp(o_o, "xO")
    p_x, p_y = send(p_o, -2, 1, "xPx"), send(p_s, -2, 0, "xPy")
    n_x, n_y = send(n_o, 2, 1, "xNx"), send(n_s, 2, 0, "xNy")
    x_o, g_o, e_o = together(first, o_s, o_x, wg, wu)
    got_o = swap_dp(e_o, "preO")
    x_p, g_p, e_p = together(first, after(p_y, g_o), p_x, wg, wu)
    got_p = swap_dp(e_p, "preP")
    x_n, g_n, e_n = together(first, after(n_y, g_p), n_x, wg, wu)
    got_n = swap_dp(e_n, "preN")
    h_o, r_o, u_o = together(middle, e_o, after(got_o, g_n), g_o, wd)
    dg_o = swap_dp(u_o, "dhO")
    h_p, r_p, u_p = together(middle, e_p, after(got_p, u_o), g_p, wd)
    dg_p = swap_dp(u_p, "dhP")
    h_n, r_n, u_n = together(middle, e_n, after(got_n, u_p), g_n, wd)
    dg_n = swap_dp(u_n, "dhN")
    a_o, os, oo = together(last, e_o, got_o, u_o, after(dg_o, u_n), wg, wu)
    o_o = swap_dp(oo, "rO")
    a_p, ps, po = together(last, e_p, got_p, u_p, after(dg_p, a_o), wg, wu)
    p_s, p_o = send(ps, 2, 0, "rPs"), send(po, 2, 1, "rPo")
    a_n, ns, no = together(last, e_n, got_n, u_n, after(dg_n, a_p), wg, wu)
    n_s, n_o = send(ns, -2, 0, "rNs"), send(no, -2, 1, "rNo")
    gg, gu, gd = grads((x_o, x_p, x_n), (a_o, a_p, a_n), (r_o, r_p, r_n), (h_o, h_p, h_n))
    d_tokens = unpack(d, after(sel, gd), (p_s, os, n_s), (p_o, o_o, n_o))
    return (d_tokens, gg[None], gu[None], gd[None])


def solution(mesh):
    return jax.shard_map(
        per_device,
        mesh=mesh,
        in_specs=(
            P(("blk", "dp"), None),
            P(("blk", "dp"), None),
            P(("blk", "dp"), None),
            P("blk", "dp", None),
            P("blk", "dp", None),
            P("blk", "dp", None),
        ),
        out_specs=(
            P(("blk", "dp"), None),
            P("blk", "dp", None),
            P("blk", "dp", None),
            P("blk", "dp", None),
        ),
        check_vma=False,
    )
```

time: 431 us -> 115 us (0.27)
  waiting for transfers between devices: 300 us -> 23.3 us
  Pallas kernels: 0 us -> 47.8 us
  matrix products: 33.7 us -> 0 us
  other arithmetic: 24.4 us -> 0 us
  between operations: 14.3 us -> 0.75 us
  local copies, waits for them, and re-layouts: 16.5 us -> 3.21 us
    all_gather x1 -> x0, waiting for transfers between devices: 107 us -> none  [sent_together(): lax.all_gather(both, axis, axis=dim, tiled=True)]
    reduce_scatter x1 -> x0, waiting for transfers between devices: 105 us -> none  [side_by_side(): lax.psum_scatter(both, axis, scatter_dimension=dim, tiled=True)]
    ppermute x12 -> x28, waiting for transfers between devices: 88.6 us -> 23.3 us  [the longest x12 15.4 us: swap_core(): lax.ppermute(x, 'blk', [(i, i ^ 1) for i in range(lax.axis_size('blk'))])]
    pallas_call x0 -> x18, Pallas kernels: none -> 47.8 us  [the longest x3 11.1 us: pre(): pl.pallas_call(pre_kernel, out_shape=(jax.ShapeDtypeStruct((rows, width),...]
    dot_general x12 -> x0, matrix products: 33.7 us -> none  [the longest x3 13.4 us: matmul(): return jnp.dot(left_side, right_side, preferred_element_type=jnp.float32)]
    concatenate x4 -> x0, other arithmetic: 22.6 us -> none  [the longest x1 14.7 us: side_by_side(): both = jnp.concatenate(arrays, axis=along)]
    unnamed x25 -> x18, local copies, waits for them, and re-layouts: 10.7 us -> 3.2 us
    broadcast_in_dim x1 -> x0, local copies, waits for them, and re-layouts: 4.79 us -> none  [per_device(): grad_down = summed_down.astype(jnp.bfloat16)[None]]
  transfers between devices with their start and end apart: 14 -> 28, of which waited for: 13 -> 14; matrix products, arithmetic and copies ran while one was open for 3% -> 0% of each run, Pallas kernels for 0% -> 40%
where the time goes in v1:
time: 115 us; the launch traced here: 114 us
  Pallas kernels  47.8 us (42%)
  starting transfers between devices  38.9 us (34%)
  waiting for transfers between devices  23.3 us (20%)
  local copies, waits for them, and re-layouts  3.21 us (3%)
    ppermute x8, starting transfers between devices, send(): return lax.ppermute(x, ('blk', 'dp'), route)  24.6 us
    ppermute x12, waiting for transfers between devices, swap_core(): lax.ppermute(x, 'blk', [(i, i ^ 1) for i in range(lax.axis_size('blk'))])  15.4 us
    pallas_call x3, Pallas kernels, pre(): pl.pallas_call(pre_kernel, out_shape=(jax.ShapeDtypeStruct((rows, width),...  11.1 us
    pallas_call x3, Pallas kernels, back(): pl.pallas_call(back_kernel, out_shape=(jax.ShapeDtypeStruct((rows, 2 * f)...  9.96 us
    pallas_call x1, Pallas kernels, grads(): pl.pallas_call(functools.partial(grads_kernel, (len(xs), len(acts), len(b...  9.85 us
    ppermute x8, waiting for transfers between devices, send(): return lax.ppermute(x, ('blk', 'dp'), route)  7.95 us
    ppermute x12, starting transfers between devices, swap_core(): lax.ppermute(x, 'blk', [(i, i ^ 1) for i in range(lax.axis_size('blk'))])  7.84 us
    pallas_call x3, Pallas kernels, down(): pl.pallas_call(down_kernel, out_shape=(jax.ShapeDtypeStruct((rows, f), BF...  7.48 us
  transfers between devices with their start and end apart: 28, of which 14 were waited for; matrix products, arithmetic and copies ran while one was open for 0% of the time, Pallas kernels for 40%

profile of v1, /device:TPU:1, one launch (start us, length us, event | category | flops | bytes accessed | tf_op | source)
XLA Modules:
  0.0 114.1 jit_solution(307963124625031829)
XLA Ops:
  0.6 1.2 %copy-done = bf16[128,3584]{1,0:T(8,128)(2,1)S(1)} copy-done((bf16[128,3584]{1,0:T(8,128)(2,1)S(1)}, bf16[128,3584]{1,0:T(8,128)(2,1)}, u32[]{:S(2)}) %copy-start) | copy-done | bytes 917528
  1.8 0.7 copy-done.1
  2.5 0.7 copy-done.2
  3.1 0.6 select.1
  3.8 2.1 %collective-permute-start.12 = (bf16[64,1920]{1,0:T(8,128)(2,1)S(1)}, bf16[64,1920]{1,0:T(8,128)(2,1)S(1)}, u32[]{:S(2)}, u32[]{:S(2)}) collective-permute-start(bf16[64,1920]{1,0:T(8,128)(2,1)S(1)} %get-tuple-element.205), channel_id=1, source_target_pairs={{0,1},{1,0},{2,3},{3,2},{4,5},{5,4},{6,7},{7,6},{8,9},{9,8},{10,11... | collective-permute-start | bytes 737288 | tf_op jit(solution)/shard_map/xO/ppermute | solution.py:39
  5.9 10.2 %collective-permute-start.13 = (bf16[64,1920]{1,0:T(8,128)(2,1)S(1)}, bf16[64,1920]{1,0:T(8,128)(2,1)S(1)}, u32[]{:S(2)}, u32[]{:S(2)}) collective-permute-start(bf16[64,1920]{1,0:T(8,128)(2,1)S(1)} %get-tuple-element.207), channel_id=1, source_target_pairs={{0,252},{1,253},{2,254},{3,255},{4,0},{5,1},{6,2},{7,3},{8,4},{9,5... | collective-permute-start | bytes 737288 | tf_op jit(solution)/shard_map/xPy/ppermute | solution.py:34
  16.3 1.5 %collective-permute-start.15 = (bf16[64,1920]{1,0:T(8,128)(2,1)S(1)}, bf16[64,1920]{1,0:T(8,128)(2,1)S(1)}, u32[]{:S(2)}, u32[]{:S(2)}) collective-permute-start(bf16[64,1920]{1,0:T(8,128)(2,1)S(1)} %get-tuple-element.212), channel_id=1, source_target_pairs={{0,4},{1,5},{2,6},{3,7},{4,8},{5,9},{6,10},{7,11},{8,12},{9,13},{1... | collective-permute-start | bytes 737288 | tf_op jit(solution)/shard_map/xNy/ppermute | solution.py:34
  17.8 6.8 %conditional.9 = ((bf16[256,1792]{1,0:T(8,128)(2,1)}, bf16[256,128]{1,0:T(8,128)(2,1)S(1)}, bf16[256,1024]{1,0:T(8,128)(2,1)S(1)})) conditional(s32[]{:T(128)} %convert_element_type.2, () %tuple.86, (bf16[64,1920]{1,0:T(8,128)(2,1)S(1)}, bf16[64,1920]{1,0:T(8,128)(2,1)S(1)}, bf16[1792,512]{1,0:T(8,128)(2,1)}, bf16[1792,512]{1,0:T(8,128)(2,1)}) %tuple.144), branch_computations={%region_0.0_spmd, %region_1.0_spmd} | conditional | bytes 1966168 | solution.py:283
  17.8 1.8 %collective-permute-start = (bf16[64,1920]{1,0:T(8,128)(2,1)S(1)}, bf16[64,1920]{1,0:T(8,128)(2,1)S(1)}, u32[]{:S(2)}, u32[]{:S(2)}) collective-permute-start(bf16[64,1920]{1,0:T(8,128)(2,1)S(1)} %get-tuple-element.84.a), channel_id=1, source_target_pairs={{0,2},{2,0},{4,6},{6,4},{8,10},{10,8},{12,14},{14,12},{16,18},{18,... | collective-permute-start | bytes 737288 | tf_op jit(solution)/shard_map/cond/branch_1_fun/cs/ppermute | solution.py:44
  19.6 1.1 collective-permute-done.c
  20.8 0.4 collective-permute-done.1.d
  21.1 3.5 %pre.3 = (bf16[256,1792]{1,0:T(8,128)(2,1)}, bf16[256,128]{1,0:T(8,128)(2,1)S(1)}, bf16[256,1024]{1,0:T(8,128)(2,1)S(1)}) custom-call(bf16[64,1920]{1,0:T(8,128)(2,1)S(1)} %get-tuple-element.84.a, bf16[64,1920]{1,0:T(8,128)(2,1)S(1)} %get-tuple-element.85.b, bf16[64,1920]{1,0:T(8,128)(2,1)S(1)} %collective-permute-done.c, ...), custom_call_target="tpu_custom_call" | custom-call | tf_op jit(solution)/shard_map/cond/branch_1_fun/pre/pallas_call | solution.py:109
  24.6 0.7 collective-permute-start.16
  25.3 0.9 collective-permute-start.17
  26.1 3.5 %collective-permute-done.14 = bf16[64,1920]{1,0:T(8,128)(2,1)S(1)} collective-permute-done((bf16[64,1920]{1,0:T(8,128)(2,1)S(1)}, bf16[64,1920]{1,0:T(8,128)(2,1)S(1)}, u32[]{:S(2)}, u32[]{:S(2)}) %collective-permute-start.14) | collective-permute-done | bytes 245792 | tf_op jit(solution)/shard_map/xPx/ppermute | solution.py:34
  29.6 6.6 %conditional.10 = ((bf16[256,1792]{1,0:T(8,128)(2,1)}, bf16[256,128]{1,0:T(8,128)(2,1)}, bf16[256,1024]{1,0:T(8,128)(2,1)S(1)})) conditional(s32[]{:T(128)} %convert_element_type.2, () %tuple.88, (bf16[64,1920]{1,0:T(8,128)(2,1)S(1)}, bf16[64,1920]{1,0:T(8,128)(2,1)S(1)}, bf16[1792,512]{1,0:T(8,128)(2,1)}, bf16[1792,512]{1,0:T(8,128)(2,1)}) %tuple.145), branch_computations={%region_2.0_spmd, %region_3.0_spmd} | conditional | bytes 1966168 | solution.py:283
  29.6 1.4 %collective-permute-start.2 = (bf16[64,1920]{1,0:T(8,128)(2,1)S(1)}, bf16[64,1920]{1,0:T(8,128)(2,1)S(1)}, u32[]{:S(2)}, u32[]{:S(2)}) collective-permute-start(bf16[64,1920]{1,0:T(8,128)(2,1)S(1)} %get-tuple-element.88.a), channel_id=1, source_target_pairs={{0,2},{2,0},{4,6},{6,4},{8,10},{10,8},{12,14},{14,12},{16,18},{18,... | collective-permute-start | bytes 737288 | tf_op jit(solution)/shard_map/cond/branch_1_fun/cs/ppermute | solution.py:44
  31.1 1.1 collective-permute-done.2.c
  32.2 0.4 collective-permute-done.3.d
  32.6 3.7 %pre.4 = (bf16[256,1792]{1,0:T(8,128)(2,1)}, bf16[256,128]{1,0:T(8,128)(2,1)}, bf16[256,1024]{1,0:T(8,128)(2,1)S(1)}) custom-call(bf16[64,1920]{1,0:T(8,128)(2,1)S(1)} %get-tuple-element.88.a, bf16[64,1920]{1,0:T(8,128)(2,1)S(1)} %get-tuple-element.89.b, bf16[64,1920]{1,0:T(8,128)(2,1)S(1)} %collective-permute-done.2.c, ...), custom_call_target="tpu_custom_call" | custom-call | tf_op jit(solution)/shard_map/cond/branch_1_fun/pre/pallas_call | solution.py:109
  36.3 4.5 %collective-permute-done.16 = bf16[64,1920]{1,0:T(8,128)(2,1)S(1)} collective-permute-done((bf16[64,1920]{1,0:T(8,128)(2,1)S(1)}, bf16[64,1920]{1,0:T(8,128)(2,1)S(1)}, u32[]{:S(2)}, u32[]{:S(2)}) %collective-permute-start.16) | collective-permute-done | bytes 245792 | tf_op jit(solution)/shard_map/xNx/ppermute | solution.py:34
  40.7 0.7 copy-done.11
  41.4 6.5 %conditional.11 = ((bf16[256,1792]{1,0:T(8,128)(2,1)}, bf16[256,128]{1,0:T(8,128)(2,1)}, bf16[256,1024]{1,0:T(8,128)(2,1)S(1)})) conditional(s32[]{:T(128)} %convert_element_type.2, () %tuple.91, (bf16[64,1920]{1,0:T(8,128)(2,1)}, bf16[64,1920]{1,0:T(8,128)(2,1)}, bf16[1792,512]{1,0:T(8,128)(2,1)}, bf16[1792,512]{1,0:T(8,128)(2,1)}) %tuple.154), branch_computations={%region_4.0_spmd, %region_5.0_spmd} | conditional | bytes 1966168 | solution.py:283
  41.4 0.9 collective-permute-start.4
  42.3 1.3 %collective-permute-done.4.c = bf16[64,1920]{1,0:T(8,128)(2,1)S(1)} collective-permute-done((bf16[64,1920]{1,0:T(8,128)(2,1)}, bf16[64,1920]{1,0:T(8,128)(2,1)S(1)}, u32[]{:S(2)}, u32[]{:S(2)}) %collective-permute-start.4) | collective-permute-done | bytes 245792 | tf_op jit(solution)/shard_map/cond/branch_1_fun/cs/ppermute | solution.py:44
  44.0 3.9 %pre.5 = (bf16[256,1792]{1,0:T(8,128)(2,1)}, bf16[256,128]{1,0:T(8,128)(2,1)}, bf16[256,1024]{1,0:T(8,128)(2,1)S(1)}) custom-call(bf16[64,1920]{1,0:T(8,128)(2,1)} %get-tuple-element.92.a, bf16[64,1920]{1,0:T(8,128)(2,1)} %get-tuple-element.93.b, bf16[64,1920]{1,0:T(8,128)(2,1)S(1)} %collective-permute-done.4.c, ...), custom_call_target="tpu_custom_call" | custom-call | tf_op jit(solution)/shard_map/cond/branch_1_fun/pre/pallas_call | solution.py:109
  48.0 6.6 %conditional.12 = (bf16[256,512]{1,0:T(8,128)(2,1)}, bf16[256,1792]{1,0:T(8,128)(2,1)}, bf16[256,512]{1,0:T(8,128)(2,1)}) conditional(s32[]{:T(128)} %convert_element_type.2, () %tuple.95, (bf16[256,1024]{1,0:T(8,128)(2,1)S(1)}, bf16[256,1024]{1,0:T(8,128)(2,1)}, bf16[1792,512]{1,0:T(8,128)(2,1)S(1)}, bf16[256,128]{1,0:T(8,128)(2,1)S(1)}) %tuple.151), branch_computations={%region_6.0_spmd, %region_7.0_spmd} | conditional | bytes 3670080 | solution.py:283
  48.0 2.3 %down.3 = (bf16[256,512]{1,0:T(8,128)(2,1)}, bf16[256,1792]{1,0:T(8,128)(2,1)S(1)}) custom-call(bf16[256,1024]{1,0:T(8,128)(2,1)S(1)} %get-tuple-element.96.sent, bf16[256,1024]{1,0:T(8,128)(2,1)} %get-tuple-element.97.got, bf16[1792,512]{1,0:T(8,128)(2,1)S(1)} %get-tuple-element.98.wd), custom_call_target="tpu_custom_call" | custom-call | tf_op jit(solution)/shard_map/cond/branch_1_fun/down/pallas_call | solution.py:136
  50.3 0.6 collective-permute-start.6
  50.9 2.1 %collective-permute-done.6.got = bf16[256,1792]{1,0:T(8,128)(2,1)S(1)} collective-permute-done((bf16[256,1792]{1,0:T(8,128)(2,1)S(1)}, bf16[256,1792]{1,0:T(8,128)(2,1)S(1)}, u32[]{:S(2)}, u32[]{:S(2)}) %collective-permute-start.6) | collective-permute-done | bytes 917536 | tf_op jit(solution)/shard_map/cond/branch_1_fun/eo/ppermute | solution.py:44
  53.0 1.6 %turn.3 = (bf16[256,1792]{1,0:T(8,128)(2,1)}, bf16[256,512]{1,0:T(8,128)(2,1)}) custom-call(bf16[256,1792]{1,0:T(8,128)(2,1)S(1)} %get-tuple-element.100.part, bf16[256,1792]{1,0:T(8,128)(2,1)S(1)} %collective-permute-done.6.got, bf16[256,128]{1,0:T(8,128)(2,1)S(1)} %get-tuple-element.101.gates, bf16[1792,512]{1,0:T(8,128)(2,1)S(1)} %get-tuple-element.98.wd), custom_call_target="tpu_custom_call" | custom-call | tf_op jit(solution)/shard_map/cond/branch_1_fun/turn/pallas_call | solution.py:160
  54.6 1.5 %collective-permute-start.18 = (bf16[256,512]{1,0:T(8,128)(2,1)}, bf16[256,512]{1,0:T(8,128)(2,1)}, u32[]{:S(2)}, u32[]{:S(2)}) collective-permute-start(bf16[256,512]{1,0:T(8,128)(2,1)} %get-tuple-element.220), channel_id=1, source_target_pairs={{0,1},{1,0},{2,3},{3,2},{4,5},{5,4},{6,7},{7,6},{8,9},{9,8},{10,11... | collective-permute-start | bytes 786440 | tf_op jit(solution)/shard_map/dhO/ppermute | solution.py:39
  56.1 6.8 %conditional.13 = (bf16[256,512]{1,0:T(8,128)(2,1)}, bf16[256,1792]{1,0:T(8,128)(2,1)}, bf16[256,512]{1,0:T(8,128)(2,1)}) conditional(s32[]{:T(128)} %convert_element_type.2, () %tuple.99, (bf16[256,1024]{1,0:T(8,128)(2,1)S(1)}, bf16[256,1024]{1,0:T(8,128)(2,1)}, bf16[1792,512]{1,0:T(8,128)(2,1)S(1)}, bf16[256,128]{1,0:T(8,128)(2,1)}) %tuple.152), branch_computations={%region_8.0_spmd, %region_9.0_spmd} | conditional | bytes 3932252 | solution.py:283
  56.1 2.4 %down.4 = (bf16[256,512]{1,0:T(8,128)(2,1)}, bf16[256,1792]{1,0:T(8,128)(2,1)S(1)}) custom-call(bf16[256,1024]{1,0:T(8,128)(2,1)S(1)} %get-tuple-element.104.sent, bf16[256,1024]{1,0:T(8,128)(2,1)} %get-tuple-element.105.got, bf16[1792,512]{1,0:T(8,128)(2,1)S(1)} %get-tuple-element.106.wd), custom_call_target="tpu_custom_call" | custom-call | tf_op jit(solution)/shard_map/cond/branch_1_fun/down/pallas_call | solution.py:136
  58.5 0.7 collective-permute-start.7
  59.1 2.1 %collective-permute-done.7.got = bf16[256,1792]{1,0:T(8,128)(2,1)S(1)} collective-permute-done((bf16[256,1792]{1,0:T(8,128)(2,1)S(1)}, bf16[256,1792]{1,0:T(8,128)(2,1)S(1)}, u32[]{:S(2)}, u32[]{:S(2)}) %collective-permute-start.7) | collective-permute-done | bytes 917536 | tf_op jit(solution)/shard_map/cond/branch_1_fun/eo/ppermute | solution.py:44
  61.2 1.6 %turn.4 = (bf16[256,1792]{1,0:T(8,128)(2,1)}, bf16[256,512]{1,0:T(8,128)(2,1)}) custom-call(bf16[256,1792]{1,0:T(8,128)(2,1)S(1)} %get-tuple-element.108.part, bf16[256,1792]{1,0:T(8,128)(2,1)S(1)} %collective-permute-done.7.got, bf16[256,128]{1,0:T(8,128)(2,1)S(1)} %copy-done.8, bf16[1792,512]{1,0:T(8,128)(2,1)S(1)} %get-tuple-element.106.wd), custom_call_target="tpu_custom_call" | custom-call | tf_op jit(solution)/shard_map/cond/branch_1_fun/turn/pallas_call | solution.py:160
  62.9 7.1 %conditional.14 = (bf16[256,512]{1,0:T(8,128)(2,1)}, bf16[256,1792]{1,0:T(8,128)(2,1)}, bf16[256,512]{1,0:T(8,128)(2,1)}) conditional(s32[]{:T(128)} %convert_element_type.2, () %tuple.98, (bf16[256,1024]{1,0:T(8,128)(2,1)S(1)}, bf16[256,1024]{1,0:T(8,128)(2,1)}, bf16[1792,512]{1,0:T(8,128)(2,1)}, bf16[256,128]{1,0:T(8,128)(2,1)}) %tuple.150), branch_computations={%region_10.0_spmd, %region_11.0_spmd} | conditional | bytes 11272312 | solution.py:283
  62.9 2.8 %down.5 = (bf16[256,512]{1,0:T(8,128)(2,1)}, bf16[256,1792]{1,0:T(8,128)(2,1)S(1)}) custom-call(bf16[256,1024]{1,0:T(8,128)(2,1)S(1)} %get-tuple-element.112.sent, bf16[256,1024]{1,0:T(8,128)(2,1)} %get-tuple-element.113.got, bf16[1792,512]{1,0:T(8,128)(2,1)} %get-tuple-element.114.wd), custom_call_target="tpu_custom_call" | custom-call | tf_op jit(solution)/shard_map/cond/branch_1_fun/down/pallas_call | solution.py:136
  65.6 0.6 collective-permute-start.8
  66.2 2.1 %collective-permute-done.8.got = bf16[256,1792]{1,0:T(8,128)(2,1)S(1)} collective-permute-done((bf16[256,1792]{1,0:T(8,128)(2,1)S(1)}, bf16[256,1792]{1,0:T(8,128)(2,1)S(1)}, u32[]{:S(2)}, u32[]{:S(2)}) %collective-permute-start.8) | collective-permute-done | bytes 917536 | tf_op jit(solution)/shard_map/cond/branch_1_fun/eo/ppermute | solution.py:44
  68.3 1.7 %turn.5 = (bf16[256,1792]{1,0:T(8,128)(2,1)}, bf16[256,512]{1,0:T(8,128)(2,1)}) custom-call(bf16[256,1792]{1,0:T(8,128)(2,1)S(1)} %get-tuple-element.116.part, bf16[256,1792]{1,0:T(8,128)(2,1)S(1)} %collective-permute-done.8.got, bf16[256,128]{1,0:T(8,128)(2,1)S(1)} %copy-done.9, bf16[1792,512]{1,0:T(8,128)(2,1)S(1)} %copy-done.5), custom_call_target="tpu_custom_call" | custom-call | tf_op jit(solution)/shard_map/cond/branch_1_fun/turn/pallas_call | solution.py:160
  70.0 1.5 %collective-permute-start.22 = (bf16[256,512]{1,0:T(8,128)(2,1)}, bf16[256,512]{1,0:T(8,128)(2,1)}, u32[]{:S(2)}, u32[]{:S(2)}) collective-permute-start(bf16[256,512]{1,0:T(8,128)(2,1)} %get-tuple-element.226), channel_id=1, source_target_pairs={{0,1},{1,0},{2,3},{3,2},{4,5},{5,4},{6,7},{7,6},{8,9},{9,8},{10,11... | collective-permute-start | bytes 786440 | tf_op jit(solution)/shard_map/dhN/ppermute | solution.py:39
  71.5 6.2 %conditional.15 = (bf16[256,1024]{1,0:T(8,128)(2,1)}, bf16[64,1792]{1,0:T(8,128)(2,1)}, bf16[64,1792]{1,0:T(8,128)(2,1)}) conditional(s32[]{:T(128)} %convert_element_type.2, () %tuple.94, (bf16[256,1024]{1,0:T(8,128)(2,1)S(1)}, bf16[256,1024]{1,0:T(8,128)(2,1)}, bf16[256,512]{1,0:T(8,128)(2,1)}, bf16[256,512]{1,0:T(8,128)(2,1)}, ...), branch_computations={%region_12.0_spmd, %region_13.0_spmd} | conditional | bytes 1835072 | solution.py:283
  71.5 3.3 %back.3 = (bf16[256,1024]{1,0:T(8,128)(2,1)}, bf16[128,1792]{1,0:T(8,128)(2,1)S(1)}, bf16[128,1792]{1,0:T(8,128)(2,1)S(1)}) custom-call(bf16[256,1024]{1,0:T(8,128)(2,1)S(1)} %get-tuple-element.120.sent, bf16[256,1024]{1,0:T(8,128)(2,1)} %get-tuple-element.121.got, bf16[256,512]{1,0:T(8,128)(2,1)} %get-tuple-element.122.dh_sent, ...), custom_call_target="tpu_custom_call" | custom-call | tf_op jit(solution)/shard_map/cond/branch_1_fun/back/pallas_call | solution.py:191
  74.8 0.7 collective-permute-start.9
  75.5 1.4 %collective-permute-done.9.got = bf16[128,1792]{1,0:T(8,128)(2,1)S(1)} collective-permute-done((bf16[128,1792]{1,0:T(8,128)(2,1)S(1)}, bf16[128,1792]{1,0:T(8,128)(2,1)S(1)}, u32[]{:S(2)}, u32[]{:S(2)}) %collective-permute-start.9) | collective-permute-done | bytes 458784 | tf_op jit(solution)/shard_map/cond/branch_1_fun/dx/ppermute | solution.py:44
  76.9 0.8 add.3
  77.7 6.0 %conditional.16 = (bf16[256,1024]{1,0:T(8,128)(2,1)}, bf16[64,1792]{1,0:T(8,128)(2,1)}, bf16[64,1792]{1,0:T(8,128)(2,1)}) conditional(s32[]{:T(128)} %convert_element_type.2, () %tuple.106, (bf16[256,1024]{1,0:T(8,128)(2,1)S(1)}, bf16[256,1024]{1,0:T(8,128)(2,1)}, bf16[256,512]{1,0:T(8,128)(2,1)}, bf16[256,512]{1,0:T(8,128)(2,1)}, ...), branch_computations={%region_14.0_spmd, %region_15.0_spmd} | conditional | bytes 1835072 | solution.py:283
  77.7 3.3 %back.4 = (bf16[256,1024]{1,0:T(8,128)(2,1)}, bf16[128,1792]{1,0:T(8,128)(2,1)S(1)}, bf16[128,1792]{1,0:T(8,128)(2,1)S(1)}) custom-call(bf16[256,1024]{1,0:T(8,128)(2,1)S(1)} %get-tuple-element.131.sent, bf16[256,1024]{1,0:T(8,128)(2,1)} %get-tuple-element.132.got, bf16[256,512]{1,0:T(8,128)(2,1)} %get-tuple-element.133.dh_sent, ...), custom_call_target="tpu_custom_call" | custom-call | tf_op jit(solution)/shard_map/cond/branch_1_fun/back/pallas_call | solution.py:191
  81.1 0.4 collective-permute-start.10
  81.4 1.4 %collective-permute-done.10.got = bf16[128,1792]{1,0:T(8,128)(2,1)S(1)} collective-permute-done((bf16[128,1792]{1,0:T(8,128)(2,1)S(1)}, bf16[128,1792]{1,0:T(8,128)(2,1)S(1)}, u32[]{:S(2)}, u32[]{:S(2)}) %collective-permute-start.10) | collective-permute-done | bytes 458784 | tf_op jit(solution)/shard_map/cond/branch_1_fun/dx/ppermute | solution.py:44
  82.9 0.9 add.4
  83.7 2.7 %collective-permute-start.23 = (bf16[64,1792]{1,0:T(8,128)(2,1)}, bf16[64,1792]{1,0:T(8,128)(2,1)S(1)}, u32[]{:S(2)}, u32[]{:S(2)}) collective-permute-start(bf16[64,1792]{1,0:T(8,128)(2,1)} %get-tuple-element.241), channel_id=1, source_target_pairs={{0,4},{1,5},{2,6},{3,7},{4,8},{5,9},{6,10},{7,11},{8,12},{9,13},{1... | collective-permute-start | bytes 688136 | tf_op jit(solution)/shard_map/rPs/ppermute | solution.py:34
  86.5 0.4 collective-permute-start.26
  86.9 6.6 %conditional.17 = (bf16[256,1024]{1,0:T(8,128)(2,1)}, bf16[64,1792]{1,0:T(8,128)(2,1)}, bf16[64,1792]{1,0:T(8,128)(2,1)}) conditional(s32[]{:T(128)} %convert_element_type.2, () %tuple.109, (bf16[256,1024]{1,0:T(8,128)(2,1)S(1)}, bf16[256,1024]{1,0:T(8,128)(2,1)}, bf16[256,512]{1,0:T(8,128)(2,1)}, bf16[256,512]{1,0:T(8,128)(2,1)}, ...), branch_computations={%region_16.0_spmd, %region_17.0_spmd} | conditional | bytes 1835072 | solution.py:283
  86.9 3.3 %back.5 = (bf16[256,1024]{1,0:T(8,128)(2,1)}, bf16[128,1792]{1,0:T(8,128)(2,1)S(1)}, bf16[128,1792]{1,0:T(8,128)(2,1)S(1)}) custom-call(bf16[256,1024]{1,0:T(8,128)(2,1)S(1)} %get-tuple-element.142.sent, bf16[256,1024]{1,0:T(8,128)(2,1)} %get-tuple-element.143.got, bf16[256,512]{1,0:T(8,128)(2,1)} %get-tuple-element.144.dh_sent, ...), custom_call_target="tpu_custom_call" | custom-call | tf_op jit(solution)/shard_map/cond/branch_1_fun/back/pallas_call | solution.py:191
  90.2 0.9 collective-permute-start.11
  91.2 1.4 %collective-permute-done.11.got = bf16[128,1792]{1,0:T(8,128)(2,1)S(1)} collective-permute-done((bf16[128,1792]{1,0:T(8,128)(2,1)S(1)}, bf16[128,1792]{1,0:T(8,128)(2,1)S(1)}, u32[]{:S(2)}, u32[]{:S(2)}) %collective-permute-start.11) | collective-permute-done | bytes 458784 | tf_op jit(solution)/shard_map/cond/branch_1_fun/dx/ppermute | solution.py:44
  92.6 0.8 add.5
  93.5 7.9 %collective-permute-start.24 = (bf16[64,1792]{1,0:T(8,128)(2,1)}, bf16[64,1792]{1,0:T(8,128)(2,1)S(1)}, u32[]{:S(2)}, u32[]{:S(2)}) collective-permute-start(bf16[64,1792]{1,0:T(8,128)(2,1)} %get-tuple-element.243), channel_id=1, source_target_pairs={{0,252},{1,253},{2,254},{3,255},{4,0},{5,1},{6,2},{7,3},{8,4},{9,5... | collective-permute-start | bytes 688136 | tf_op jit(solution)/shard_map/rNs/ppermute | solution.py:34
  101.4 1.4 %collective-permute-start.27 = (bf16[64,1792]{1,0:T(8,128)(2,1)}, bf16[64,1792]{1,0:T(8,128)(2,1)S(1)}, u32[]{:S(2)}, u32[]{:S(2)}) collective-permute-start(bf16[64,1792]{1,0:T(8,128)(2,1)} %get-tuple-element.246), channel_id=1, source_target_pairs={{0,253},{1,252},{2,255},{3,254},{4,1},{5,0},{6,3},{7,2},{8,5},{9,4... | collective-permute-start | bytes 688136 | tf_op jit(solution)/shard_map/rNo/ppermute | solution.py:34
  102.8 9.8 %grads.1 = (bf16[1792,512]{1,0:T(8,128)(2,1)}, bf16[1792,512]{1,0:T(8,128)(2,1)}, bf16[1792,512]{1,0:T(8,128)(2,1)}) custom-call(bf16[256,1792]{1,0:T(8,128)(2,1)} %get-tuple-element.206.refs_0_, bf16[256,1792]{1,0:T(8,128)(2,1)} %get-tuple-element.211.refs_1_, bf16[256,1792]{1,0:T(8,128)(2,1)} %get-tuple-element.216.refs_2_, ...), custom_call_target="tpu_custom_call" | custom-call | tf_op jit(solution)/shard_map/grads/pallas_call | solution.py:258
  112.7 1.4 %unpack.1 = bf16[128,3584]{1,0:T(8,128)(2,1)} custom-call(s32[1]{0:T(128)} %bitcast.d_ref, bf16[192,128]{1,0:T(8,128)(2,1)S(1)} %get-tuple-element.240.sel, bf16[64,1792]{1,0:T(8,128)(2,1)S(1)} %collective-permute-done.23.s0, bf16[64,1792]{1,0:T(8,128)(2,1)S(1)} %copy-done.7, bf16[64,1792]{1,0:T(8,128)(2,1)S(1)} %collective-permute-done.24.s2, ...), custom_call_target="tpu_custom_call" | custom-call | tf_op jit(solution)/shard_map/unpack/pallas_call | solution.py:224
  (43 shorter events, 0.7 us)
Async XLA Ops:
  0.6 1.2 %copy-start = (bf16[128,3584]{1,0:T(8,128)(2,1)S(1)}, bf16[128,3584]{1,0:T(8,128)(2,1)}, u32[]{:S(2)}) copy-start(bf16[128,3584]{1,0:T(8,128)(2,1)} %tokens.1) | copy-start | bytes 2752516
  1.8 0.7 copy-start.1
  2.5 0.7 copy-start.2
  3.8 14.1 %collective-permute-start.12 = (bf16[64,1920]{1,0:T(8,128)(2,1)S(1)}, bf16[64,1920]{1,0:T(8,128)(2,1)S(1)}, u32[]{:S(2)}, u32[]{:S(2)}) collective-permute-start(bf16[64,1920]{1,0:T(8,128)(2,1)S(1)} %get-tuple-element.205), channel_id=1, source_target_pairs={{0,1},{1,0},{2,3},{3,2},{4,5},{5,4},{6,7},{7,6},{8,9},{9,8},{10,11... | collective-permute-start | bytes 737288 | tf_op jit(solution)/shard_map/xO/ppermute | solution.py:39
  5.9 20.2 %collective-permute-start.13 = (bf16[64,1920]{1,0:T(8,128)(2,1)S(1)}, bf16[64,1920]{1,0:T(8,128)(2,1)S(1)}, u32[]{:S(2)}, u32[]{:S(2)}) collective-permute-start(bf16[64,1920]{1,0:T(8,128)(2,1)S(1)} %get-tuple-element.207), channel_id=1, source_target_pairs={{0,252},{1,253},{2,254},{3,255},{4,0},{5,1},{6,2},{7,3},{8,4},{9,5... | collective-permute-start | bytes 737288 | tf_op jit(solution)/shard_map/xPy/ppermute | solution.py:34
  16.1 13.5 %collective-permute-start.14 = (bf16[64,1920]{1,0:T(8,128)(2,1)S(1)}, bf16[64,1920]{1,0:T(8,128)(2,1)S(1)}, u32[]{:S(2)}, u32[]{:S(2)}) collective-permute-start(bf16[64,1920]{1,0:T(8,128)(2,1)S(1)} %get-tuple-element.210), channel_id=1, source_target_pairs={{0,253},{1,252},{2,255},{3,254},{4,1},{5,0},{6,3},{7,2},{8,5},{9,4... | collective-permute-start | bytes 737288 | tf_op jit(solution)/shard_map/xPx/ppermute | solution.py:34
  16.3 20.0 %collective-permute-start.15 = (bf16[64,1920]{1,0:T(8,128)(2,1)S(1)}, bf16[64,1920]{1,0:T(8,128)(2,1)S(1)}, u32[]{:S(2)}, u32[]{:S(2)}) collective-permute-start(bf16[64,1920]{1,0:T(8,128)(2,1)S(1)} %get-tuple-element.212), channel_id=1, source_target_pairs={{0,4},{1,5},{2,6},{3,7},{4,8},{5,9},{6,10},{7,11},{8,12},{9,13},{1... | collective-permute-start | bytes 737288 | tf_op jit(solution)/shard_map/xNy/ppermute | solution.py:34
  17.8 2.9 %collective-permute-start = (bf16[64,1920]{1,0:T(8,128)(2,1)S(1)}, bf16[64,1920]{1,0:T(8,128)(2,1)S(1)}, u32[]{:S(2)}, u32[]{:S(2)}) collective-permute-start(bf16[64,1920]{1,0:T(8,128)(2,1)S(1)} %get-tuple-element.84.a), channel_id=1, source_target_pairs={{0,2},{2,0},{4,6},{6,4},{8,10},{10,8},{12,14},{14,12},{16,18},{18,... | collective-permute-start | bytes 737288 | tf_op jit(solution)/shard_map/cond/branch_1_fun/cs/ppermute | solution.py:44
  19.6 1.5 %collective-permute-start.1 = (bf16[64,1920]{1,0:T(8,128)(2,1)S(1)}, bf16[64,1920]{1,0:T(8,128)(2,1)S(1)}, u32[]{:S(2)}, u32[]{:S(2)}) collective-permute-start(bf16[64,1920]{1,0:T(8,128)(2,1)S(1)} %get-tuple-element.85.b), channel_id=1, source_target_pairs={{0,2},{2,0},{4,6},{6,4},{8,10},{10,8},{12,14},{14,12},{16,18},{18,... | collective-permute-start | bytes 737288 | tf_op jit(solution)/shard_map/cond/branch_1_fun/cx/ppermute | solution.py:44
  24.6 16.1 %collective-permute-start.16 = (bf16[64,1920]{1,0:T(8,128)(2,1)S(1)}, bf16[64,1920]{1,0:T(8,128)(2,1)S(1)}, u32[]{:S(2)}, u32[]{:S(2)}) collective-permute-start(bf16[64,1920]{1,0:T(8,128)(2,1)S(1)} %get-tuple-element.215), channel_id=1, source_target_pairs={{0,5},{1,4},{2,7},{3,6},{4,9},{5,8},{6,11},{7,10},{8,13},{9,12},{1... | collective-permute-start | bytes 737288 | tf_op jit(solution)/shard_map/xNx/ppermute | solution.py:34
  25.3 22.7 %collective-permute-start.17 = (bf16[256,1024]{1,0:T(8,128)(2,1)S(1)}, bf16[256,1024]{1,0:T(8,128)(2,1)}, u32[]{:S(2)}, u32[]{:S(2)}) collective-permute-start(bf16[256,1024]{1,0:T(8,128)(2,1)S(1)} %get-tuple-element.217), channel_id=1, source_target_pairs={{0,1},{1,0},{2,3},{3,2},{4,5},{5,4},{6,7},{7,6},{8,9},{9,8},{10,11... | collective-permute-start | bytes 1572872 | tf_op jit(solution)/shard_map/preO/ppermute | solution.py:39
  29.6 2.6 %collective-permute-start.2 = (bf16[64,1920]{1,0:T(8,128)(2,1)S(1)}, bf16[64,1920]{1,0:T(8,128)(2,1)S(1)}, u32[]{:S(2)}, u32[]{:S(2)}) collective-permute-start(bf16[64,1920]{1,0:T(8,128)(2,1)S(1)} %get-tuple-element.88.a), channel_id=1, source_target_pairs={{0,2},{2,0},{4,6},{6,4},{8,10},{10,8},{12,14},{14,12},{16,18},{18,... | collective-permute-start | bytes 737288 | tf_op jit(solution)/shard_map/cond/branch_1_fun/cs/ppermute | solution.py:44
  31.0 1.5 %collective-permute-start.3 = (bf16[64,1920]{1,0:T(8,128)(2,1)S(1)}, bf16[64,1920]{1,0:T(8,128)(2,1)S(1)}, u32[]{:S(2)}, u32[]{:S(2)}) collective-permute-start(bf16[64,1920]{1,0:T(8,128)(2,1)S(1)} %get-tuple-element.89.b), channel_id=1, source_target_pairs={{0,2},{2,0},{4,6},{6,4},{8,10},{10,8},{12,14},{14,12},{16,18},{18,... | collective-permute-start | bytes 737288 | tf_op jit(solution)/shard_map/cond/branch_1_fun/cx/ppermute | solution.py:44
  36.2 19.9 %collective-permute-start.20 = (bf16[256,1024]{1,0:T(8,128)(2,1)S(1)}, bf16[256,1024]{1,0:T(8,128)(2,1)}, u32[]{:S(2)}, u32[]{:S(2)}) collective-permute-start(bf16[256,1024]{1,0:T(8,128)(2,1)S(1)} %get-tuple-element.222), channel_id=1, source_target_pairs={{0,1},{1,0},{2,3},{3,2},{4,5},{5,4},{6,7},{7,6},{8,9},{9,8},{10,11... | collective-permute-start | bytes 1572872 | tf_op jit(solution)/shard_map/preP/ppermute | solution.py:39
  36.2 4.5 %copy-start.10 = (bf16[64,1920]{1,0:T(8,128)(2,1)}, bf16[64,1920]{1,0:T(8,128)(2,1)S(1)}, u32[]{:S(2)}) copy-start(bf16[64,1920]{1,0:T(8,128)(2,1)S(1)} %collective-permute-done.15) | copy-start | bytes 737284
  40.7 0.7 copy-start.11
  41.4 6.5 %copy-start.4 = (bf16[1,1792,512]{2,1,0:T(8,128)(2,1)S(1)}, bf16[1,1792,512]{2,1,0:T(8,128)(2,1)}, u32[]{:S(2)}) copy-start(bf16[1,1792,512]{2,1,0:T(8,128)(2,1)} %param.29) | copy-start | bytes 5505028
  41.4 2.2 %collective-permute-start.4 = (bf16[64,1920]{1,0:T(8,128)(2,1)}, bf16[64,1920]{1,0:T(8,128)(2,1)S(1)}, u32[]{:S(2)}, u32[]{:S(2)}) collective-permute-start(bf16[64,1920]{1,0:T(8,128)(2,1)} %get-tuple-element.92.a), channel_id=1, source_target_pairs={{0,2},{2,0},{4,6},{6,4},{8,10},{10,8},{12,14},{14,12},{16,18},{18,... | collective-permute-start | bytes 737288 | tf_op jit(solution)/shard_map/cond/branch_1_fun/cs/ppermute | solution.py:44
  42.3 1.7 %collective-permute-start.5 = (bf16[64,1920]{1,0:T(8,128)(2,1)}, bf16[64,1920]{1,0:T(8,128)(2,1)S(1)}, u32[]{:S(2)}, u32[]{:S(2)}) collective-permute-start(bf16[64,1920]{1,0:T(8,128)(2,1)} %get-tuple-element.93.b), channel_id=1, source_target_pairs={{0,2},{2,0},{4,6},{6,4},{8,10},{10,8},{12,14},{14,12},{16,18},{18,... | collective-permute-start | bytes 737288 | tf_op jit(solution)/shard_map/cond/branch_1_fun/cx/ppermute | solution.py:44
  47.9 14.9 %collective-permute-start.19 = (bf16[256,1024]{1,0:T(8,128)(2,1)S(1)}, bf16[256,1024]{1,0:T(8,128)(2,1)}, u32[]{:S(2)}, u32[]{:S(2)}) collective-permute-start(bf16[256,1024]{1,0:T(8,128)(2,1)S(1)} %get-tuple-element.221), channel_id=1, source_target_pairs={{0,1},{1,0},{2,3},{3,2},{4,5},{5,4},{6,7},{7,6},{8,9},{9,8},{10,11... | collective-permute-start | bytes 1572872 | tf_op jit(solution)/shard_map/preN/ppermute | solution.py:39
  50.3 2.7 %collective-permute-start.6 = (bf16[256,1792]{1,0:T(8,128)(2,1)S(1)}, bf16[256,1792]{1,0:T(8,128)(2,1)S(1)}, u32[]{:S(2)}, u32[]{:S(2)}) collective-permute-start(bf16[256,1792]{1,0:T(8,128)(2,1)S(1)} %get-tuple-element.100.part), channel_id=1, source_target_pairs={{0,2},{2,0},{4,6},{6,4},{8,10},{10,8},{12,14},{14,12},{16,18},{18,... | collective-permute-start | bytes 2752520 | tf_op jit(solution)/shard_map/cond/branch_1_fun/eo/ppermute | solution.py:44
  54.6 17.0 %collective-permute-start.18 = (bf16[256,512]{1,0:T(8,128)(2,1)}, bf16[256,512]{1,0:T(8,128)(2,1)}, u32[]{:S(2)}, u32[]{:S(2)}) collective-permute-start(bf16[256,512]{1,0:T(8,128)(2,1)} %get-tuple-element.220), channel_id=1, source_target_pairs={{0,1},{1,0},{2,3},{3,2},{4,5},{5,4},{6,7},{7,6},{8,9},{9,8},{10,11... | collective-permute-start | bytes 786440 | tf_op jit(solution)/shard_map/dhO/ppermute | solution.py:39
  56.1 5.1 %copy-start.8 = (bf16[256,128]{1,0:T(8,128)(2,1)S(1)}, bf16[256,128]{1,0:T(8,128)(2,1)}, u32[]{:S(2)}) copy-start(bf16[256,128]{1,0:T(8,128)(2,1)} %get-tuple-element.109.gates) | copy-start | bytes 196612 | tf_op jit(solution)/shard_map/cond
  58.5 2.8 %collective-permute-start.7 = (bf16[256,1792]{1,0:T(8,128)(2,1)S(1)}, bf16[256,1792]{1,0:T(8,128)(2,1)S(1)}, u32[]{:S(2)}, u32[]{:S(2)}) collective-permute-start(bf16[256,1792]{1,0:T(8,128)(2,1)S(1)} %get-tuple-element.108.part), channel_id=1, source_target_pairs={{0,2},{2,0},{4,6},{6,4},{8,10},{10,8},{12,14},{14,12},{16,18},{18,... | collective-permute-start | bytes 2752520 | tf_op jit(solution)/shard_map/cond/branch_1_fun/eo/ppermute | solution.py:44
  62.8 14.9 %collective-permute-start.21 = (bf16[256,512]{1,0:T(8,128)(2,1)}, bf16[256,512]{1,0:T(8,128)(2,1)}, u32[]{:S(2)}, u32[]{:S(2)}) collective-permute-start(bf16[256,512]{1,0:T(8,128)(2,1)} %get-tuple-element.224), channel_id=1, source_target_pairs={{0,1},{1,0},{2,3},{3,2},{4,5},{5,4},{6,7},{7,6},{8,9},{9,8},{10,11... | collective-permute-start | bytes 786440 | tf_op jit(solution)/shard_map/dhP/ppermute | solution.py:39
  62.8 8.7 %copy-start.3 = (bf16[1,1792,512]{2,1,0:T(8,128)(2,1)S(1)}, bf16[1,1792,512]{2,1,0:T(8,128)(2,1)}, u32[]{:S(2)}) copy-start(bf16[1,1792,512]{2,1,0:T(8,128)(2,1)} %param.27) | copy-start | bytes 5505028
  62.9 5.4 %copy-start.5 = (bf16[1792,512]{1,0:T(8,128)(2,1)S(1)}, bf16[1792,512]{1,0:T(8,128)(2,1)}, u32[]{:S(2)}) copy-start(bf16[1792,512]{1,0:T(8,128)(2,1)} %get-tuple-element.114.wd) | copy-start | bytes 5505028 | tf_op jit(solution)/shard_map/cond
  62.9 5.4 %copy-start.9 = (bf16[256,128]{1,0:T(8,128)(2,1)S(1)}, bf16[256,128]{1,0:T(8,128)(2,1)}, u32[]{:S(2)}) copy-start(bf16[256,128]{1,0:T(8,128)(2,1)} %get-tuple-element.117.gates) | copy-start | bytes 196612 | tf_op jit(solution)/shard_map/cond
  65.6 2.7 %collective-permute-start.8 = (bf16[256,1792]{1,0:T(8,128)(2,1)S(1)}, bf16[256,1792]{1,0:T(8,128)(2,1)S(1)}, u32[]{:S(2)}, u32[]{:S(2)}) collective-permute-start(bf16[256,1792]{1,0:T(8,128)(2,1)S(1)} %get-tuple-element.116.part), channel_id=1, source_target_pairs={{0,2},{2,0},{4,6},{6,4},{8,10},{10,8},{12,14},{14,12},{16,18},{18,... | collective-permute-start | bytes 2752520 | tf_op jit(solution)/shard_map/cond/branch_1_fun/eo/ppermute | solution.py:44
  70.0 16.9 %collective-permute-start.22 = (bf16[256,512]{1,0:T(8,128)(2,1)}, bf16[256,512]{1,0:T(8,128)(2,1)}, u32[]{:S(2)}, u32[]{:S(2)}) collective-permute-start(bf16[256,512]{1,0:T(8,128)(2,1)} %get-tuple-element.226), channel_id=1, source_target_pairs={{0,1},{1,0},{2,3},{3,2},{4,5},{5,4},{6,7},{7,6},{8,9},{9,8},{10,11... | collective-permute-start | bytes 786440 | tf_op jit(solution)/shard_map/dhN/ppermute | solution.py:39
  74.8 2.1 %collective-permute-start.9 = (bf16[128,1792]{1,0:T(8,128)(2,1)S(1)}, bf16[128,1792]{1,0:T(8,128)(2,1)S(1)}, u32[]{:S(2)}, u32[]{:S(2)}) collective-permute-start(bf16[128,1792]{1,0:T(8,128)(2,1)S(1)} %get-tuple-element.128), channel_id=1, source_target_pairs={{0,2},{2,0},{4,6},{6,4},{8,10},{10,8},{12,14},{14,12},{16,18},{18,... | collective-permute-start | bytes 1376264 | tf_op jit(solution)/shard_map/cond/branch_1_fun/dx/ppermute | solution.py:44
  81.1 1.8 %collective-permute-start.10 = (bf16[128,1792]{1,0:T(8,128)(2,1)S(1)}, bf16[128,1792]{1,0:T(8,128)(2,1)S(1)}, u32[]{:S(2)}, u32[]{:S(2)}) collective-permute-start(bf16[128,1792]{1,0:T(8,128)(2,1)S(1)} %get-tuple-element.139), channel_id=1, source_target_pairs={{0,2},{2,0},{4,6},{6,4},{8,10},{10,8},{12,14},{14,12},{16,18},{18,... | collective-permute-start | bytes 1376264 | tf_op jit(solution)/shard_map/cond/branch_1_fun/dx/ppermute | solution.py:44
  83.7 28.9 %collective-permute-start.23 = (bf16[64,1792]{1,0:T(8,128)(2,1)}, bf16[64,1792]{1,0:T(8,128)(2,1)S(1)}, u32[]{:S(2)}, u32[]{:S(2)}) collective-permute-start(bf16[64,1792]{1,0:T(8,128)(2,1)} %get-tuple-element.241), channel_id=1, source_target_pairs={{0,4},{1,5},{2,6},{3,7},{4,8},{5,9},{6,10},{7,11},{8,12},{9,13},{1... | collective-permute-start | bytes 688136 | tf_op jit(solution)/shard_map/rPs/ppermute | solution.py:34
  86.5 26.2 %collective-permute-start.25 = (bf16[64,1792]{1,0:T(8,128)(2,1)}, bf16[64,1792]{1,0:T(8,128)(2,1)S(1)}, u32[]{:S(2)}, u32[]{:S(2)}) collective-permute-start(bf16[64,1792]{1,0:T(8,128)(2,1)} %get-tuple-element.244), channel_id=1, source_target_pairs={{0,5},{1,4},{2,7},{3,6},{4,9},{5,8},{6,11},{7,10},{8,13},{9,12},{1... | collective-permute-start | bytes 688136 | tf_op jit(solution)/shard_map/rPo/ppermute | solution.py:34
  86.5 26.2 %collective-permute-start.26 = (bf16[64,1792]{1,0:T(8,128)(2,1)}, bf16[64,1792]{1,0:T(8,128)(2,1)S(1)}, u32[]{:S(2)}, u32[]{:S(2)}) collective-permute-start(bf16[64,1792]{1,0:T(8,128)(2,1)} %get-tuple-element.245), channel_id=1, source_target_pairs={{0,1},{1,0},{2,3},{3,2},{4,5},{5,4},{6,7},{7,6},{8,9},{9,8},{10,11... | collective-permute-start | bytes 688136 | tf_op jit(solution)/shard_map/rO/ppermute | solution.py:39
  86.9 15.9 %copy-start.6 = (bf16[256,512]{1,0:T(8,128)(2,1)S(1)}, bf16[256,512]{1,0:T(8,128)(2,1)}, u32[]{:S(2)}) copy-start(bf16[256,512]{1,0:T(8,128)(2,1)} %get-tuple-element.236.refs_9_) | copy-start | bytes 786436
  90.2 2.4 %collective-permute-start.11 = (bf16[128,1792]{1,0:T(8,128)(2,1)S(1)}, bf16[128,1792]{1,0:T(8,128)(2,1)S(1)}, u32[]{:S(2)}, u32[]{:S(2)}) collective-permute-start(bf16[128,1792]{1,0:T(8,128)(2,1)S(1)} %get-tuple-element.150), channel_id=1, source_target_pairs={{0,2},{2,0},{4,6},{6,4},{8,10},{10,8},{12,14},{14,12},{16,18},{18,... | collective-permute-start | bytes 1376264 | tf_op jit(solution)/shard_map/cond/branch_1_fun/dx/ppermute | solution.py:44
  93.5 19.2 %collective-permute-start.24 = (bf16[64,1792]{1,0:T(8,128)(2,1)}, bf16[64,1792]{1,0:T(8,128)(2,1)S(1)}, u32[]{:S(2)}, u32[]{:S(2)}) collective-permute-start(bf16[64,1792]{1,0:T(8,128)(2,1)} %get-tuple-element.243), channel_id=1, source_target_pairs={{0,252},{1,253},{2,254},{3,255},{4,0},{5,1},{6,2},{7,3},{8,4},{9,5... | collective-permute-start | bytes 688136 | tf_op jit(solution)/shard_map/rNs/ppermute | solution.py:34
  101.4 11.3 %collective-permute-start.27 = (bf16[64,1792]{1,0:T(8,128)(2,1)}, bf16[64,1792]{1,0:T(8,128)(2,1)S(1)}, u32[]{:S(2)}, u32[]{:S(2)}) collective-permute-start(bf16[64,1792]{1,0:T(8,128)(2,1)} %get-tuple-element.246), channel_id=1, source_target_pairs={{0,253},{1,252},{2,255},{3,254},{4,1},{5,0},{6,3},{7,2},{8,5},{9,4... | collective-permute-start | bytes 688136 | tf_op jit(solution)/shard_map/rNo/ppermute | solution.py:34
  102.8 9.9 %copy-start.7 = (bf16[64,1792]{1,0:T(8,128)(2,1)S(1)}, bf16[64,1792]{1,0:T(8,128)(2,1)}, u32[]{:S(2)}) copy-start(bf16[64,1792]{1,0:T(8,128)(2,1)} %get-tuple-element.242.s1) | copy-start | bytes 688132

commit v2 on v1

--- a/solution.py
+++ b/solution.py
@@ -12,7 +12,7 @@
 BF16 = jnp.bfloat16
 F32 = jnp.float32
 PARAMS = pltpu.CompilerParams(vmem_limit_bytes=20 * 1024 * 1024)
-SMALL = pltpu.CompilerParams(vmem_limit_bytes=12 * 1024 * 1024)
+SMALL = pltpu.CompilerParams(vmem_limit_bytes=10 * 1024 * 1024)
 
 
 def dot(a, b):
@@ -94,13 +94,49 @@
     return reorder(sent[...]).astype(F32) + got[...].astype(F32)
 
 
-def pre_kernel(a, b, c, d, wg, wu, x_out, gates, out):
+STREAMS = 4
+
+
+def fetch(pairs, sems):
+    copies = []
+    for i, (src, dst) in enumerate(pairs):
+        n = src.shape[0] // STREAMS
+        group = [
+            pltpu.make_async_copy(
+                src.at[pl.ds(j * n, n)], dst.at[pl.ds(j * n, n)], sems.at[i * STREAMS + j]
+            )
+            for j in range(STREAMS)
+        ]
+        for copy in group:
+            copy.start()
+        copies.append(group)
+    return copies
+
+
+def arrived(group):
+    for copy in group:
+        copy.wait()
+
+
+def weight_specs(inputs, weights):
+    return [pl.BlockSpec(memory_space=pltpu.VMEM)] * inputs + [
+        pl.BlockSpec(memory_space=pltpu.HBM)
+    ] * weights
+
+
+def weight_scratch(w, n):
+    return [pltpu.VMEM(w.shape, BF16)] * n + [pltpu.SemaphoreType.DMA((n * STREAMS,))]
+
+
+def pre_kernel(a, b, c, d, wg_in, wu_in, x_out, gates, out, wg, wu, sems):
+    copies = fetch(((wg_in, wg), (wu_in, wu)), sems)
     width, f = wg.shape
     pieces = (a, b, c, d)
     x = jnp.concatenate([p[:, :width] for p in pieces], axis=0)
     x_out[...] = x
     gates[...] = jnp.concatenate([p[:, width:] for p in pieces], axis=0)
     for k, w in enumerate((wg, wu)):
+        arrived(copies[k])
         out[:, k * f : (k + 1) * f] = reorder(dot(x, w[...]).astype(BF16))
 
 
@@ -113,6 +149,8 @@
             jax.ShapeDtypeStruct((rows, EXTRA), BF16),
             jax.ShapeDtypeStruct((rows, 2 * f), BF16),
         ),
+        in_specs=weight_specs(4, 2),
+        scratch_shapes=weight_scratch(wg, 2),
         compiler_params=SMALL,
         name="pre",
     )(*pieces, wg, wu)

time: 115 us -> 114 us (level)
  no operation moved by 1% of the time
where the time goes in v2:
time: 114 us
  Pallas kernels  47.1 us (41%)
  starting transfers between devices  39.1 us (34%)
  waiting for transfers between devices  23.7 us (21%)
  local copies, waits for them, and re-layouts  3.21 us (3%)
    ppermute x8, starting transfers between devices, send(): return lax.ppermute(x, ('blk', 'dp'), route)  24.2 us
    ppermute x12, waiting for transfers between devices, swap_core(): lax.ppermute(x, 'blk', [(i, i ^ 1) for i in range(lax.axis_size('blk'))])  15.4 us
    pallas_call x3, Pallas kernels, pre(): pl.pallas_call(pre_kernel, out_shape=(jax.ShapeDtypeStruct((rows, width),...  10.3 us
    pallas_call x3, Pallas kernels, back(): pl.pallas_call(back_kernel, out_shape=(jax.ShapeDtypeStruct((rows, 2 * f)...  9.95 us
    pallas_call x1, Pallas kernels, grads(): pl.pallas_call(functools.partial(grads_kernel, (len(xs), len(acts), len(b...  9.91 us
    ppermute x8, waiting for transfers between devices, send(): return lax.ppermute(x, ('blk', 'dp'), route)  8.33 us
    ppermute x12, starting transfers between devices, swap_core(): lax.ppermute(x, 'blk', [(i, i ^ 1) for i in range(lax.axis_size('blk'))])  7.91 us
    pallas_call x3, Pallas kernels, down(): pl.pallas_call(down_kernel, out_shape=(jax.ShapeDtypeStruct((rows, f), BF...  7.48 us
  transfers between devices with their start and end apart: 28, of which 14 were waited for; matrix products, arithmetic and copies ran while one was open for 0% of the time, Pallas kernels for 40%

profile of v2, /device:TPU:1, one launch (start us, length us, event | category | flops | bytes accessed | tf_op | source)
XLA Modules:
  0.0 113.9 jit_solution(8969153452198490373)
XLA Ops:
  0.6 1.2 %copy-done = bf16[128,3584]{1,0:T(8,128)(2,1)S(1)} copy-done((bf16[128,3584]{1,0:T(8,128)(2,1)S(1)}, bf16[128,3584]{1,0:T(8,128)(2,1)}, u32[]{:S(2)}) %copy-start) | copy-done | bytes 917528
  1.8 0.7 copy-done.1
  2.5 0.7 copy-done.2
  3.1 0.6 select.1
  3.8 2.1 %collective-permute-start.12 = (bf16[64,1920]{1,0:T(8,128)(2,1)S(1)}, bf16[64,1920]{1,0:T(8,128)(2,1)S(1)}, u32[]{:S(2)}, u32[]{:S(2)}) collective-permute-start(bf16[64,1920]{1,0:T(8,128)(2,1)S(1)} %get-tuple-element.205), channel_id=1, source_target_pairs={{0,1},{1,0},{2,3},{3,2},{4,5},{5,4},{6,7},{7,6},{8,9},{9,8},{10,11... | collective-permute-start | bytes 737288 | tf_op jit(solution)/shard_map/xO/ppermute | solution.py:39
  5.9 10.2 %collective-permute-start.13 = (bf16[64,1920]{1,0:T(8,128)(2,1)S(1)}, bf16[64,1920]{1,0:T(8,128)(2,1)S(1)}, u32[]{:S(2)}, u32[]{:S(2)}) collective-permute-start(bf16[64,1920]{1,0:T(8,128)(2,1)S(1)} %get-tuple-element.207), channel_id=1, source_target_pairs={{0,252},{1,253},{2,254},{3,255},{4,0},{5,1},{6,2},{7,3},{8,4},{9,5... | collective-permute-start | bytes 737288 | tf_op jit(solution)/shard_map/xPy/ppermute | solution.py:34
  16.3 1.5 %collective-permute-start.15 = (bf16[64,1920]{1,0:T(8,128)(2,1)S(1)}, bf16[64,1920]{1,0:T(8,128)(2,1)S(1)}, u32[]{:S(2)}, u32[]{:S(2)}) collective-permute-start(bf16[64,1920]{1,0:T(8,128)(2,1)S(1)} %get-tuple-element.212), channel_id=1, source_target_pairs={{0,4},{1,5},{2,6},{3,7},{4,8},{5,9},{6,10},{7,11},{8,12},{9,13},{1... | collective-permute-start | bytes 737288 | tf_op jit(solution)/shard_map/xNy/ppermute | solution.py:34
  17.8 6.4 %conditional.9 = ((bf16[256,1792]{1,0:T(8,128)(2,1)}, bf16[256,128]{1,0:T(8,128)(2,1)S(1)}, bf16[256,1024]{1,0:T(8,128)(2,1)S(1)})) conditional(s32[]{:T(128)} %convert_element_type.2, () %tuple.86, (bf16[64,1920]{1,0:T(8,128)(2,1)S(1)}, bf16[64,1920]{1,0:T(8,128)(2,1)S(1)}, bf16[1792,512]{1,0:T(8,128)(2,1)}, bf16[1792,512]{1,0:T(8,128)(2,1)}) %tuple.144), branch_computations={%region_0.0_spmd, %region_1.0_spmd} | conditional | bytes 1966168 | solution.py:321
  17.8 1.8 %collective-permute-start = (bf16[64,1920]{1,0:T(8,128)(2,1)S(1)}, bf16[64,1920]{1,0:T(8,128)(2,1)S(1)}, u32[]{:S(2)}, u32[]{:S(2)}) collective-permute-start(bf16[64,1920]{1,0:T(8,128)(2,1)S(1)} %get-tuple-element.84.a), channel_id=1, source_target_pairs={{0,2},{2,0},{4,6},{6,4},{8,10},{10,8},{12,14},{14,12},{16,18},{18,... | collective-permute-start | bytes 737288 | tf_op jit(solution)/shard_map/cond/branch_1_fun/cs/ppermute | solution.py:44
  19.6 1.1 collective-permute-done.c
  20.8 0.4 collective-permute-done.1.d
  21.1 3.1 %pre.3 = (bf16[256,1792]{1,0:T(8,128)(2,1)}, bf16[256,128]{1,0:T(8,128)(2,1)S(1)}, bf16[256,1024]{1,0:T(8,128)(2,1)S(1)}) custom-call(bf16[64,1920]{1,0:T(8,128)(2,1)S(1)} %get-tuple-element.84.a, bf16[64,1920]{1,0:T(8,128)(2,1)S(1)} %get-tuple-element.85.b, bf16[64,1920]{1,0:T(8,128)(2,1)S(1)} %collective-permute-done.c, ...), custom_call_target="tpu_custom_call" | custom-call | tf_op jit(solution)/shard_map/cond/branch_1_fun/pre/pallas_call | solution.py:145
  24.2 0.7 collective-permute-start.16
  25.0 1.0 collective-permute-start.17
  25.9 3.7 %collective-permute-done.14 = bf16[64,1920]{1,0:T(8,128)(2,1)S(1)} collective-permute-done((bf16[64,1920]{1,0:T(8,128)(2,1)S(1)}, bf16[64,1920]{1,0:T(8,128)(2,1)S(1)}, u32[]{:S(2)}, u32[]{:S(2)}) %collective-permute-start.14) | collective-permute-done | bytes 245792 | tf_op jit(solution)/shard_map/xPx/ppermute | solution.py:34
  29.6 6.0 %conditional.10 = ((bf16[256,1792]{1,0:T(8,128)(2,1)}, bf16[256,128]{1,0:T(8,128)(2,1)}, bf16[256,1024]{1,0:T(8,128)(2,1)S(1)})) conditional(s32[]{:T(128)} %convert_element_type.2, () %tuple.88, (bf16[64,1920]{1,0:T(8,128)(2,1)S(1)}, bf16[64,1920]{1,0:T(8,128)(2,1)S(1)}, bf16[1792,512]{1,0:T(8,128)(2,1)}, bf16[1792,512]{1,0:T(8,128)(2,1)}) %tuple.145), branch_computations={%region_2.0_spmd, %region_3.0_spmd} | conditional | bytes 1966168 | solution.py:321
  29.6 1.4 %collective-permute-start.2 = (bf16[64,1920]{1,0:T(8,128)(2,1)S(1)}, bf16[64,1920]{1,0:T(8,128)(2,1)S(1)}, u32[]{:S(2)}, u32[]{:S(2)}) collective-permute-start(bf16[64,1920]{1,0:T(8,128)(2,1)S(1)} %get-tuple-element.88.a), channel_id=1, source_target_pairs={{0,2},{2,0},{4,6},{6,4},{8,10},{10,8},{12,14},{14,12},{16,18},{18,... | collective-permute-start | bytes 737288 | tf_op jit(solution)/shard_map/cond/branch_1_fun/cs/ppermute | solution.py:44
  31.1 1.1 collective-permute-done.2.c
  32.2 0.4 collective-permute-done.3.d
  32.6 3.1 %pre.4 = (bf16[256,1792]{1,0:T(8,128)(2,1)}, bf16[256,128]{1,0:T(8,128)(2,1)}, bf16[256,1024]{1,0:T(8,128)(2,1)S(1)}) custom-call(bf16[64,1920]{1,0:T(8,128)(2,1)S(1)} %get-tuple-element.88.a, bf16[64,1920]{1,0:T(8,128)(2,1)S(1)} %get-tuple-element.89.b, bf16[64,1920]{1,0:T(8,128)(2,1)S(1)} %collective-permute-done.2.c, ...), custom_call_target="tpu_custom_call" | custom-call | tf_op jit(solution)/shard_map/cond/branch_1_fun/pre/pallas_call | solution.py:145
  35.8 4.7 %collective-permute-done.16 = bf16[64,1920]{1,0:T(8,128)(2,1)S(1)} collective-permute-done((bf16[64,1920]{1,0:T(8,128)(2,1)S(1)}, bf16[64,1920]{1,0:T(8,128)(2,1)S(1)}, u32[]{:S(2)}, u32[]{:S(2)}) %collective-permute-start.16) | collective-permute-done | bytes 245792 | tf_op jit(solution)/shard_map/xNx/ppermute | solution.py:34
  40.4 0.7 copy-done.11
  41.1 6.7 %conditional.11 = ((bf16[256,1792]{1,0:T(8,128)(2,1)}, bf16[256,128]{1,0:T(8,128)(2,1)}, bf16[256,1024]{1,0:T(8,128)(2,1)S(1)})) conditional(s32[]{:T(128)} %convert_element_type.2, () %tuple.91, (bf16[64,1920]{1,0:T(8,128)(2,1)}, bf16[64,1920]{1,0:T(8,128)(2,1)}, bf16[1792,512]{1,0:T(8,128)(2,1)}, bf16[1792,512]{1,0:T(8,128)(2,1)}) %tuple.154), branch_computations={%region_4.0_spmd, %region_5.0_spmd} | conditional | bytes 1966168 | solution.py:321
  41.1 0.9 collective-permute-start.4
  42.0 1.3 %collective-permute-done.4.c = bf16[64,1920]{1,0:T(8,128)(2,1)S(1)} collective-permute-done((bf16[64,1920]{1,0:T(8,128)(2,1)}, bf16[64,1920]{1,0:T(8,128)(2,1)S(1)}, u32[]{:S(2)}, u32[]{:S(2)}) %collective-permute-start.4) | collective-permute-done | bytes 245792 | tf_op jit(solution)/shard_map/cond/branch_1_fun/cs/ppermute | solution.py:44
  43.7 4.2 %pre.5 = (bf16[256,1792]{1,0:T(8,128)(2,1)}, bf16[256,128]{1,0:T(8,128)(2,1)}, bf16[256,1024]{1,0:T(8,128)(2,1)S(1)}) custom-call(bf16[64,1920]{1,0:T(8,128)(2,1)} %get-tuple-element.92.a, bf16[64,1920]{1,0:T(8,128)(2,1)} %get-tuple-element.93.b, bf16[64,1920]{1,0:T(8,128)(2,1)S(1)} %collective-permute-done.4.c, ...), custom_call_target="tpu_custom_call" | custom-call | tf_op jit(solution)/shard_map/cond/branch_1_fun/pre/pallas_call | solution.py:145
  48.2 6.6 %conditional.12 = (bf16[256,512]{1,0:T(8,128)(2,1)}, bf16[256,1792]{1,0:T(8,128)(2,1)}, bf16[256,512]{1,0:T(8,128)(2,1)}) conditional(s32[]{:T(128)} %convert_element_type.2, () %tuple.95, (bf16[256,1024]{1,0:T(8,128)(2,1)S(1)}, bf16[256,1024]{1,0:T(8,128)(2,1)}, bf16[1792,512]{1,0:T(8,128)(2,1)S(1)}, bf16[256,128]{1,0:T(8,128)(2,1)S(1)}) %tuple.151), branch_computations={%region_6.0_spmd, %region_7.0_spmd} | conditional | bytes 3670080 | solution.py:321
  48.2 2.3 %down.3 = (bf16[256,512]{1,0:T(8,128)(2,1)}, bf16[256,1792]{1,0:T(8,128)(2,1)S(1)}) custom-call(bf16[256,1024]{1,0:T(8,128)(2,1)S(1)} %get-tuple-element.96.sent, bf16[256,1024]{1,0:T(8,128)(2,1)} %get-tuple-element.97.got, bf16[1792,512]{1,0:T(8,128)(2,1)S(1)} %get-tuple-element.98.wd), custom_call_target="tpu_custom_call" | custom-call | tf_op jit(solution)/shard_map/cond/branch_1_fun/down/pallas_call | solution.py:174
  50.5 0.5 collective-permute-start.6
  51.1 2.1 %collective-permute-done.6.got = bf16[256,1792]{1,0:T(8,128)(2,1)S(1)} collective-permute-done((bf16[256,1792]{1,0:T(8,128)(2,1)S(1)}, bf16[256,1792]{1,0:T(8,128)(2,1)S(1)}, u32[]{:S(2)}, u32[]{:S(2)}) %collective-permute-start.6) | collective-permute-done | bytes 917536 | tf_op jit(solution)/shard_map/cond/branch_1_fun/eo/ppermute | solution.py:44
  53.2 1.6 %turn.3 = (bf16[256,1792]{1,0:T(8,128)(2,1)}, bf16[256,512]{1,0:T(8,128)(2,1)}) custom-call(bf16[256,1792]{1,0:T(8,128)(2,1)S(1)} %get-tuple-element.100.part, bf16[256,1792]{1,0:T(8,128)(2,1)S(1)} %collective-permute-done.6.got, bf16[256,128]{1,0:T(8,128)(2,1)S(1)} %get-tuple-element.101.gates, bf16[1792,512]{1,0:T(8,128)(2,1)S(1)} %get-tuple-element.98.wd), custom_call_target="tpu_custom_call" | custom-call | tf_op jit(solution)/shard_map/cond/branch_1_fun/turn/pallas_call | solution.py:198
  54.8 1.5 %collective-permute-start.18 = (bf16[256,512]{1,0:T(8,128)(2,1)}, bf16[256,512]{1,0:T(8,128)(2,1)}, u32[]{:S(2)}, u32[]{:S(2)}) collective-permute-start(bf16[256,512]{1,0:T(8,128)(2,1)} %get-tuple-element.220), channel_id=1, source_target_pairs={{0,1},{1,0},{2,3},{3,2},{4,5},{5,4},{6,7},{7,6},{8,9},{9,8},{10,11... | collective-permute-start | bytes 786440 | tf_op jit(solution)/shard_map/dhO/ppermute | solution.py:39
  56.3 6.8 %conditional.13 = (bf16[256,512]{1,0:T(8,128)(2,1)}, bf16[256,1792]{1,0:T(8,128)(2,1)}, bf16[256,512]{1,0:T(8,128)(2,1)}) conditional(s32[]{:T(128)} %convert_element_type.2, () %tuple.99, (bf16[256,1024]{1,0:T(8,128)(2,1)S(1)}, bf16[256,1024]{1,0:T(8,128)(2,1)}, bf16[1792,512]{1,0:T(8,128)(2,1)S(1)}, bf16[256,128]{1,0:T(8,128)(2,1)}) %tuple.152), branch_computations={%region_8.0_spmd, %region_9.0_spmd} | conditional | bytes 3932252 | solution.py:321
  56.3 2.4 %down.4 = (bf16[256,512]{1,0:T(8,128)(2,1)}, bf16[256,1792]{1,0:T(8,128)(2,1)S(1)}) custom-call(bf16[256,1024]{1,0:T(8,128)(2,1)S(1)} %get-tuple-element.104.sent, bf16[256,1024]{1,0:T(8,128)(2,1)} %get-tuple-element.105.got, bf16[1792,512]{1,0:T(8,128)(2,1)S(1)} %get-tuple-element.106.wd), custom_call_target="tpu_custom_call" | custom-call | tf_op jit(solution)/shard_map/cond/branch_1_fun/down/pallas_call | solution.py:174
  58.7 0.7 collective-permute-start.7
  59.3 2.1 %collective-permute-done.7.got = bf16[256,1792]{1,0:T(8,128)(2,1)S(1)} collective-permute-done((bf16[256,1792]{1,0:T(8,128)(2,1)S(1)}, bf16[256,1792]{1,0:T(8,128)(2,1)S(1)}, u32[]{:S(2)}, u32[]{:S(2)}) %collective-permute-start.7) | collective-permute-done | bytes 917536 | tf_op jit(solution)/shard_map/cond/branch_1_fun/eo/ppermute | solution.py:44
  61.4 1.6 %turn.4 = (bf16[256,1792]{1,0:T(8,128)(2,1)}, bf16[256,512]{1,0:T(8,128)(2,1)}) custom-call(bf16[256,1792]{1,0:T(8,128)(2,1)S(1)} %get-tuple-element.108.part, bf16[256,1792]{1,0:T(8,128)(2,1)S(1)} %collective-permute-done.7.got, bf16[256,128]{1,0:T(8,128)(2,1)S(1)} %copy-done.8, bf16[1792,512]{1,0:T(8,128)(2,1)S(1)} %get-tuple-element.106.wd), custom_call_target="tpu_custom_call" | custom-call | tf_op jit(solution)/shard_map/cond/branch_1_fun/turn/pallas_call | solution.py:198
  63.1 7.1 %conditional.14 = (bf16[256,512]{1,0:T(8,128)(2,1)}, bf16[256,1792]{1,0:T(8,128)(2,1)}, bf16[256,512]{1,0:T(8,128)(2,1)}) conditional(s32[]{:T(128)} %convert_element_type.2, () %tuple.98, (bf16[256,1024]{1,0:T(8,128)(2,1)S(1)}, bf16[256,1024]{1,0:T(8,128)(2,1)}, bf16[1792,512]{1,0:T(8,128)(2,1)}, bf16[256,128]{1,0:T(8,128)(2,1)}) %tuple.150), branch_computations={%region_10.0_spmd, %region_11.0_spmd} | conditional | bytes 11272312 | solution.py:321
  63.1 2.8 %down.5 = (bf16[256,512]{1,0:T(8,128)(2,1)}, bf16[256,1792]{1,0:T(8,128)(2,1)S(1)}) custom-call(bf16[256,1024]{1,0:T(8,128)(2,1)S(1)} %get-tuple-element.112.sent, bf16[256,1024]{1,0:T(8,128)(2,1)} %get-tuple-element.113.got, bf16[1792,512]{1,0:T(8,128)(2,1)} %get-tuple-element.114.wd), custom_call_target="tpu_custom_call" | custom-call | tf_op jit(solution)/shard_map/cond/branch_1_fun/down/pallas_call | solution.py:174
  65.9 0.6 collective-permute-start.8
  66.4 2.1 %collective-permute-done.8.got = bf16[256,1792]{1,0:T(8,128)(2,1)S(1)} collective-permute-done((bf16[256,1792]{1,0:T(8,128)(2,1)S(1)}, bf16[256,1792]{1,0:T(8,128)(2,1)S(1)}, u32[]{:S(2)}, u32[]{:S(2)}) %collective-permute-start.8) | collective-permute-done | bytes 917536 | tf_op jit(solution)/shard_map/cond/branch_1_fun/eo/ppermute | solution.py:44
  68.5 1.7 %turn.5 = (bf16[256,1792]{1,0:T(8,128)(2,1)}, bf16[256,512]{1,0:T(8,128)(2,1)}) custom-call(bf16[256,1792]{1,0:T(8,128)(2,1)S(1)} %get-tuple-element.116.part, bf16[256,1792]{1,0:T(8,128)(2,1)S(1)} %collective-permute-done.8.got, bf16[256,128]{1,0:T(8,128)(2,1)S(1)} %copy-done.9, bf16[1792,512]{1,0:T(8,128)(2,1)S(1)} %copy-done.5), custom_call_target="tpu_custom_call" | custom-call | tf_op jit(solution)/shard_map/cond/branch_1_fun/turn/pallas_call | solution.py:198
  70.2 1.5 %collective-permute-start.22 = (bf16[256,512]{1,0:T(8,128)(2,1)}, bf16[256,512]{1,0:T(8,128)(2,1)}, u32[]{:S(2)}, u32[]{:S(2)}) collective-permute-start(bf16[256,512]{1,0:T(8,128)(2,1)} %get-tuple-element.226), channel_id=1, source_target_pairs={{0,1},{1,0},{2,3},{3,2},{4,5},{5,4},{6,7},{7,6},{8,9},{9,8},{10,11... | collective-permute-start | bytes 786440 | tf_op jit(solution)/shard_map/dhN/ppermute | solution.py:39
  71.7 6.2 %conditional.15 = (bf16[256,1024]{1,0:T(8,128)(2,1)}, bf16[64,1792]{1,0:T(8,128)(2,1)}, bf16[64,1792]{1,0:T(8,128)(2,1)}) conditional(s32[]{:T(128)} %convert_element_type.2, () %tuple.94, (bf16[256,1024]{1,0:T(8,128)(2,1)S(1)}, bf16[256,1024]{1,0:T(8,128)(2,1)}, bf16[256,512]{1,0:T(8,128)(2,1)}, bf16[256,512]{1,0:T(8,128)(2,1)}, ...), branch_computations={%region_12.0_spmd, %region_13.0_spmd} | conditional | bytes 1835072 | solution.py:321
  71.7 3.3 %back.3 = (bf16[256,1024]{1,0:T(8,128)(2,1)}, bf16[128,1792]{1,0:T(8,128)(2,1)S(1)}, bf16[128,1792]{1,0:T(8,128)(2,1)S(1)}) custom-call(bf16[256,1024]{1,0:T(8,128)(2,1)S(1)} %get-tuple-element.120.sent, bf16[256,1024]{1,0:T(8,128)(2,1)} %get-tuple-element.121.got, bf16[256,512]{1,0:T(8,128)(2,1)} %get-tuple-element.122.dh_sent, ...), custom_call_target="tpu_custom_call" | custom-call | tf_op jit(solution)/shard_map/cond/branch_1_fun/back/pallas_call | solution.py:229
  75.0 0.7 collective-permute-start.9
  75.7 1.4 %collective-permute-done.9.got = bf16[128,1792]{1,0:T(8,128)(2,1)S(1)} collective-permute-done((bf16[128,1792]{1,0:T(8,128)(2,1)S(1)}, bf16[128,1792]{1,0:T(8,128)(2,1)S(1)}, u32[]{:S(2)}, u32[]{:S(2)}) %collective-permute-start.9) | collective-permute-done | bytes 458784 | tf_op jit(solution)/shard_map/cond/branch_1_fun/dx/ppermute | solution.py:44
  77.1 0.8 add.3
  78.0 6.0 %conditional.16 = (bf16[256,1024]{1,0:T(8,128)(2,1)}, bf16[64,1792]{1,0:T(8,128)(2,1)}, bf16[64,1792]{1,0:T(8,128)(2,1)}) conditional(s32[]{:T(128)} %convert_element_type.2, () %tuple.106, (bf16[256,1024]{1,0:T(8,128)(2,1)S(1)}, bf16[256,1024]{1,0:T(8,128)(2,1)}, bf16[256,512]{1,0:T(8,128)(2,1)}, bf16[256,512]{1,0:T(8,128)(2,1)}, ...), branch_computations={%region_14.0_spmd, %region_15.0_spmd} | conditional | bytes 1835072 | solution.py:321
  78.0 3.3 %back.4 = (bf16[256,1024]{1,0:T(8,128)(2,1)}, bf16[128,1792]{1,0:T(8,128)(2,1)S(1)}, bf16[128,1792]{1,0:T(8,128)(2,1)S(1)}) custom-call(bf16[256,1024]{1,0:T(8,128)(2,1)S(1)} %get-tuple-element.131.sent, bf16[256,1024]{1,0:T(8,128)(2,1)} %get-tuple-element.132.got, bf16[256,512]{1,0:T(8,128)(2,1)} %get-tuple-element.133.dh_sent, ...), custom_call_target="tpu_custom_call" | custom-call | tf_op jit(solution)/shard_map/cond/branch_1_fun/back/pallas_call | solution.py:229
  81.3 0.4 collective-permute-start.10
  81.7 1.4 %collective-permute-done.10.got = bf16[128,1792]{1,0:T(8,128)(2,1)S(1)} collective-permute-done((bf16[128,1792]{1,0:T(8,128)(2,1)S(1)}, bf16[128,1792]{1,0:T(8,128)(2,1)S(1)}, u32[]{:S(2)}, u32[]{:S(2)}) %collective-permute-start.10) | collective-permute-done | bytes 458784 | tf_op jit(solution)/shard_map/cond/branch_1_fun/dx/ppermute | solution.py:44
  83.1 0.9 add.4
  84.0 2.2 %collective-permute-start.23 = (bf16[64,1792]{1,0:T(8,128)(2,1)}, bf16[64,1792]{1,0:T(8,128)(2,1)S(1)}, u32[]{:S(2)}, u32[]{:S(2)}) collective-permute-start(bf16[64,1792]{1,0:T(8,128)(2,1)} %get-tuple-element.241), channel_id=1, source_target_pairs={{0,4},{1,5},{2,6},{3,7},{4,8},{5,9},{6,10},{7,11},{8,12},{9,13},{1... | collective-permute-start | bytes 688136 | tf_op jit(solution)/shard_map/rPs/ppermute | solution.py:34
  86.2 0.4 collective-permute-start.26
  86.6 6.6 %conditional.17 = (bf16[256,1024]{1,0:T(8,128)(2,1)}, bf16[64,1792]{1,0:T(8,128)(2,1)}, bf16[64,1792]{1,0:T(8,128)(2,1)}) conditional(s32[]{:T(128)} %convert_element_type.2, () %tuple.109, (bf16[256,1024]{1,0:T(8,128)(2,1)S(1)}, bf16[256,1024]{1,0:T(8,128)(2,1)}, bf16[256,512]{1,0:T(8,128)(2,1)}, bf16[256,512]{1,0:T(8,128)(2,1)}, ...), branch_computations={%region_16.0_spmd, %region_17.0_spmd} | conditional | bytes 1835072 | solution.py:321
  86.6 3.3 %back.5 = (bf16[256,1024]{1,0:T(8,128)(2,1)}, bf16[128,1792]{1,0:T(8,128)(2,1)S(1)}, bf16[128,1792]{1,0:T(8,128)(2,1)S(1)}) custom-call(bf16[256,1024]{1,0:T(8,128)(2,1)S(1)} %get-tuple-element.142.sent, bf16[256,1024]{1,0:T(8,128)(2,1)} %get-tuple-element.143.got, bf16[256,512]{1,0:T(8,128)(2,1)} %get-tuple-element.144.dh_sent, ...), custom_call_target="tpu_custom_call" | custom-call | tf_op jit(solution)/shard_map/cond/branch_1_fun/back/pallas_call | solution.py:229
  89.9 1.0 collective-permute-start.11
  90.9 1.4 %collective-permute-done.11.got = bf16[128,1792]{1,0:T(8,128)(2,1)S(1)} collective-permute-done((bf16[128,1792]{1,0:T(8,128)(2,1)S(1)}, bf16[128,1792]{1,0:T(8,128)(2,1)S(1)}, u32[]{:S(2)}, u32[]{:S(2)}) %collective-permute-start.11) | collective-permute-done | bytes 458784 | tf_op jit(solution)/shard_map/cond/branch_1_fun/dx/ppermute | solution.py:44
  92.4 0.8 add.5
  93.2 7.9 %collective-permute-start.24 = (bf16[64,1792]{1,0:T(8,128)(2,1)}, bf16[64,1792]{1,0:T(8,128)(2,1)S(1)}, u32[]{:S(2)}, u32[]{:S(2)}) collective-permute-start(bf16[64,1792]{1,0:T(8,128)(2,1)} %get-tuple-element.243), channel_id=1, source_target_pairs={{0,252},{1,253},{2,254},{3,255},{4,0},{5,1},{6,2},{7,3},{8,4},{9,5... | collective-permute-start | bytes 688136 | tf_op jit(solution)/shard_map/rNs/ppermute | solution.py:34
  101.1 1.5 %collective-permute-start.27 = (bf16[64,1792]{1,0:T(8,128)(2,1)}, bf16[64,1792]{1,0:T(8,128)(2,1)S(1)}, u32[]{:S(2)}, u32[]{:S(2)}) collective-permute-start(bf16[64,1792]{1,0:T(8,128)(2,1)} %get-tuple-element.246), channel_id=1, source_target_pairs={{0,253},{1,252},{2,255},{3,254},{4,1},{5,0},{6,3},{7,2},{8,5},{9,4... | collective-permute-start | bytes 688136 | tf_op jit(solution)/shard_map/rNo/ppermute | solution.py:34
  102.6 9.9 %grads.1 = (bf16[1792,512]{1,0:T(8,128)(2,1)}, bf16[1792,512]{1,0:T(8,128)(2,1)}, bf16[1792,512]{1,0:T(8,128)(2,1)}) custom-call(bf16[256,1792]{1,0:T(8,128)(2,1)} %get-tuple-element.206.refs_0_, bf16[256,1792]{1,0:T(8,128)(2,1)} %get-tuple-element.211.refs_1_, bf16[256,1792]{1,0:T(8,128)(2,1)} %get-tuple-element.216.refs_2_, ...), custom_call_target="tpu_custom_call" | custom-call | tf_op jit(solution)/shard_map/grads/pallas_call | solution.py:296
  112.6 1.4 %unpack.1 = bf16[128,3584]{1,0:T(8,128)(2,1)} custom-call(s32[1]{0:T(128)} %bitcast.d_ref, bf16[192,128]{1,0:T(8,128)(2,1)S(1)} %get-tuple-element.240.sel, bf16[64,1792]{1,0:T(8,128)(2,1)S(1)} %collective-permute-done.23.s0, bf16[64,1792]{1,0:T(8,128)(2,1)S(1)} %copy-done.7, bf16[64,1792]{1,0:T(8,128)(2,1)S(1)} %collective-permute-done.24.s2, ...), custom_call_target="tpu_custom_call" | custom-call | tf_op jit(solution)/shard_map/unpack/pallas_call | solution.py:262
  (43 shorter events, 1.0 us)
Async XLA Ops:
  0.6 1.2 %copy-start = (bf16[128,3584]{1,0:T(8,128)(2,1)S(1)}, bf16[128,3584]{1,0:T(8,128)(2,1)}, u32[]{:S(2)}) copy-start(bf16[128,3584]{1,0:T(8,128)(2,1)} %tokens.1) | copy-start | bytes 2752516
  1.8 0.7 copy-start.1
  2.5 0.7 copy-start.2
  3.8 14.1 %collective-permute-start.12 = (bf16[64,1920]{1,0:T(8,128)(2,1)S(1)}, bf16[64,1920]{1,0:T(8,128)(2,1)S(1)}, u32[]{:S(2)}, u32[]{:S(2)}) collective-permute-start(bf16[64,1920]{1,0:T(8,128)(2,1)S(1)} %get-tuple-element.205), channel_id=1, source_target_pairs={{0,1},{1,0},{2,3},{3,2},{4,5},{5,4},{6,7},{7,6},{8,9},{9,8},{10,11... | collective-permute-start | bytes 737288 | tf_op jit(solution)/shard_map/xO/ppermute | solution.py:39
  5.9 20.0 %collective-permute-start.13 = (bf16[64,1920]{1,0:T(8,128)(2,1)S(1)}, bf16[64,1920]{1,0:T(8,128)(2,1)S(1)}, u32[]{:S(2)}, u32[]{:S(2)}) collective-permute-start(bf16[64,1920]{1,0:T(8,128)(2,1)S(1)} %get-tuple-element.207), channel_id=1, source_target_pairs={{0,252},{1,253},{2,254},{3,255},{4,0},{5,1},{6,2},{7,3},{8,4},{9,5... | collective-permute-start | bytes 737288 | tf_op jit(solution)/shard_map/xPy/ppermute | solution.py:34
  16.1 13.5 %collective-permute-start.14 = (bf16[64,1920]{1,0:T(8,128)(2,1)S(1)}, bf16[64,1920]{1,0:T(8,128)(2,1)S(1)}, u32[]{:S(2)}, u32[]{:S(2)}) collective-permute-start(bf16[64,1920]{1,0:T(8,128)(2,1)S(1)} %get-tuple-element.210), channel_id=1, source_target_pairs={{0,253},{1,252},{2,255},{3,254},{4,1},{5,0},{6,3},{7,2},{8,5},{9,4... | collective-permute-start | bytes 737288 | tf_op jit(solution)/shard_map/xPx/ppermute | solution.py:34
  16.3 19.5 %collective-permute-start.15 = (bf16[64,1920]{1,0:T(8,128)(2,1)S(1)}, bf16[64,1920]{1,0:T(8,128)(2,1)S(1)}, u32[]{:S(2)}, u32[]{:S(2)}) collective-permute-start(bf16[64,1920]{1,0:T(8,128)(2,1)S(1)} %get-tuple-element.212), channel_id=1, source_target_pairs={{0,4},{1,5},{2,6},{3,7},{4,8},{5,9},{6,10},{7,11},{8,12},{9,13},{1... | collective-permute-start | bytes 737288 | tf_op jit(solution)/shard_map/xNy/ppermute | solution.py:34
  17.8 2.9 %collective-permute-start = (bf16[64,1920]{1,0:T(8,128)(2,1)S(1)}, bf16[64,1920]{1,0:T(8,128)(2,1)S(1)}, u32[]{:S(2)}, u32[]{:S(2)}) collective-permute-start(bf16[64,1920]{1,0:T(8,128)(2,1)S(1)} %get-tuple-element.84.a), channel_id=1, source_target_pairs={{0,2},{2,0},{4,6},{6,4},{8,10},{10,8},{12,14},{14,12},{16,18},{18,... | collective-permute-start | bytes 737288 | tf_op jit(solution)/shard_map/cond/branch_1_fun/cs/ppermute | solution.py:44
  19.6 1.5 %collective-permute-start.1 = (bf16[64,1920]{1,0:T(8,128)(2,1)S(1)}, bf16[64,1920]{1,0:T(8,128)(2,1)S(1)}, u32[]{:S(2)}, u32[]{:S(2)}) collective-permute-start(bf16[64,1920]{1,0:T(8,128)(2,1)S(1)} %get-tuple-element.85.b), channel_id=1, source_target_pairs={{0,2},{2,0},{4,6},{6,4},{8,10},{10,8},{12,14},{14,12},{16,18},{18,... | collective-permute-start | bytes 737288 | tf_op jit(solution)/shard_map/cond/branch_1_fun/cx/ppermute | solution.py:44
  24.2 16.2 %collective-permute-start.16 = (bf16[64,1920]{1,0:T(8,128)(2,1)S(1)}, bf16[64,1920]{1,0:T(8,128)(2,1)S(1)}, u32[]{:S(2)}, u32[]{:S(2)}) collective-permute-start(bf16[64,1920]{1,0:T(8,128)(2,1)S(1)} %get-tuple-element.215), channel_id=1, source_target_pairs={{0,5},{1,4},{2,7},{3,6},{4,9},{5,8},{6,11},{7,10},{8,13},{9,12},{1... | collective-permute-start | bytes 737288 | tf_op jit(solution)/shard_map/xNx/ppermute | solution.py:34
  25.0 23.2 %collective-permute-start.17 = (bf16[256,1024]{1,0:T(8,128)(2,1)S(1)}, bf16[256,1024]{1,0:T(8,128)(2,1)}, u32[]{:S(2)}, u32[]{:S(2)}) collective-permute-start(bf16[256,1024]{1,0:T(8,128)(2,1)S(1)} %get-tuple-element.217), channel_id=1, source_target_pairs={{0,1},{1,0},{2,3},{3,2},{4,5},{5,4},{6,7},{7,6},{8,9},{9,8},{10,11... | collective-permute-start | bytes 1572872 | tf_op jit(solution)/shard_map/preO/ppermute | solution.py:39
  29.6 2.6 %collective-permute-start.2 = (bf16[64,1920]{1,0:T(8,128)(2,1)S(1)}, bf16[64,1920]{1,0:T(8,128)(2,1)S(1)}, u32[]{:S(2)}, u32[]{:S(2)}) collective-permute-start(bf16[64,1920]{1,0:T(8,128)(2,1)S(1)} %get-tuple-element.88.a), channel_id=1, source_target_pairs={{0,2},{2,0},{4,6},{6,4},{8,10},{10,8},{12,14},{14,12},{16,18},{18,... | collective-permute-start | bytes 737288 | tf_op jit(solution)/shard_map/cond/branch_1_fun/cs/ppermute | solution.py:44
  31.0 1.5 %collective-permute-start.3 = (bf16[64,1920]{1,0:T(8,128)(2,1)S(1)}, bf16[64,1920]{1,0:T(8,128)(2,1)S(1)}, u32[]{:S(2)}, u32[]{:S(2)}) collective-permute-start(bf16[64,1920]{1,0:T(8,128)(2,1)S(1)} %get-tuple-element.89.b), channel_id=1, source_target_pairs={{0,2},{2,0},{4,6},{6,4},{8,10},{10,8},{12,14},{14,12},{16,18},{18,... | collective-permute-start | bytes 737288 | tf_op jit(solution)/shard_map/cond/branch_1_fun/cx/ppermute | solution.py:44
  35.6 20.6 %collective-permute-start.20 = (bf16[256,1024]{1,0:T(8,128)(2,1)S(1)}, bf16[256,1024]{1,0:T(8,128)(2,1)}, u32[]{:S(2)}, u32[]{:S(2)}) collective-permute-start(bf16[256,1024]{1,0:T(8,128)(2,1)S(1)} %get-tuple-element.222), channel_id=1, source_target_pairs={{0,1},{1,0},{2,3},{3,2},{4,5},{5,4},{6,7},{7,6},{8,9},{9,8},{10,11... | collective-permute-start | bytes 1572872 | tf_op jit(solution)/shard_map/preP/ppermute | solution.py:39
  35.8 4.7 %copy-start.10 = (bf16[64,1920]{1,0:T(8,128)(2,1)}, bf16[64,1920]{1,0:T(8,128)(2,1)S(1)}, u32[]{:S(2)}) copy-start(bf16[64,1920]{1,0:T(8,128)(2,1)S(1)} %collective-permute-done.15) | copy-start | bytes 737284
  40.4 0.7 copy-start.11
  41.1 7.0 %copy-start.4 = (bf16[1,1792,512]{2,1,0:T(8,128)(2,1)S(1)}, bf16[1,1792,512]{2,1,0:T(8,128)(2,1)}, u32[]{:S(2)}) copy-start(bf16[1,1792,512]{2,1,0:T(8,128)(2,1)} %param.29) | copy-start | bytes 5505028
  41.1 2.2 %collective-permute-start.4 = (bf16[64,1920]{1,0:T(8,128)(2,1)}, bf16[64,1920]{1,0:T(8,128)(2,1)S(1)}, u32[]{:S(2)}, u32[]{:S(2)}) collective-permute-start(bf16[64,1920]{1,0:T(8,128)(2,1)} %get-tuple-element.92.a), channel_id=1, source_target_pairs={{0,2},{2,0},{4,6},{6,4},{8,10},{10,8},{12,14},{14,12},{16,18},{18,... | collective-permute-start | bytes 737288 | tf_op jit(solution)/shard_map/cond/branch_1_fun/cs/ppermute | solution.py:44
  42.0 1.7 %collective-permute-start.5 = (bf16[64,1920]{1,0:T(8,128)(2,1)}, bf16[64,1920]{1,0:T(8,128)(2,1)S(1)}, u32[]{:S(2)}, u32[]{:S(2)}) collective-permute-start(bf16[64,1920]{1,0:T(8,128)(2,1)} %get-tuple-element.93.b), channel_id=1, source_target_pairs={{0,2},{2,0},{4,6},{6,4},{8,10},{10,8},{12,14},{14,12},{16,18},{18,... | collective-permute-start | bytes 737288 | tf_op jit(solution)/shard_map/cond/branch_1_fun/cx/ppermute | solution.py:44
  47.9 15.2 %collective-permute-start.19 = (bf16[256,1024]{1,0:T(8,128)(2,1)S(1)}, bf16[256,1024]{1,0:T(8,128)(2,1)}, u32[]{:S(2)}, u32[]{:S(2)}) collective-permute-start(bf16[256,1024]{1,0:T(8,128)(2,1)S(1)} %get-tuple-element.221), channel_id=1, source_target_pairs={{0,1},{1,0},{2,3},{3,2},{4,5},{5,4},{6,7},{7,6},{8,9},{9,8},{10,11... | collective-permute-start | bytes 1572872 | tf_op jit(solution)/shard_map/preN/ppermute | solution.py:39
  50.5 2.6 %collective-permute-start.6 = (bf16[256,1792]{1,0:T(8,128)(2,1)S(1)}, bf16[256,1792]{1,0:T(8,128)(2,1)S(1)}, u32[]{:S(2)}, u32[]{:S(2)}) collective-permute-start(bf16[256,1792]{1,0:T(8,128)(2,1)S(1)} %get-tuple-element.100.part), channel_id=1, source_target_pairs={{0,2},{2,0},{4,6},{6,4},{8,10},{10,8},{12,14},{14,12},{16,18},{18,... | collective-permute-start | bytes 2752520 | tf_op jit(solution)/shard_map/cond/branch_1_fun/eo/ppermute | solution.py:44
  54.8 17.0 %collective-permute-start.18 = (bf16[256,512]{1,0:T(8,128)(2,1)}, bf16[256,512]{1,0:T(8,128)(2,1)}, u32[]{:S(2)}, u32[]{:S(2)}) collective-permute-start(bf16[256,512]{1,0:T(8,128)(2,1)} %get-tuple-element.220), channel_id=1, source_target_pairs={{0,1},{1,0},{2,3},{3,2},{4,5},{5,4},{6,7},{7,6},{8,9},{9,8},{10,11... | collective-permute-start | bytes 786440 | tf_op jit(solution)/shard_map/dhO/ppermute | solution.py:39
  56.3 5.1 %copy-start.8 = (bf16[256,128]{1,0:T(8,128)(2,1)S(1)}, bf16[256,128]{1,0:T(8,128)(2,1)}, u32[]{:S(2)}) copy-start(bf16[256,128]{1,0:T(8,128)(2,1)} %get-tuple-element.109.gates) | copy-start | bytes 196612 | tf_op jit(solution)/shard_map/cond
  58.7 2.8 %collective-permute-start.7 = (bf16[256,1792]{1,0:T(8,128)(2,1)S(1)}, bf16[256,1792]{1,0:T(8,128)(2,1)S(1)}, u32[]{:S(2)}, u32[]{:S(2)}) collective-permute-start(bf16[256,1792]{1,0:T(8,128)(2,1)S(1)} %get-tuple-element.108.part), channel_id=1, source_target_pairs={{0,2},{2,0},{4,6},{6,4},{8,10},{10,8},{12,14},{14,12},{16,18},{18,... | collective-permute-start | bytes 2752520 | tf_op jit(solution)/shard_map/cond/branch_1_fun/eo/ppermute | solution.py:44
  63.1 14.9 %collective-permute-start.21 = (bf16[256,512]{1,0:T(8,128)(2,1)}, bf16[256,512]{1,0:T(8,128)(2,1)}, u32[]{:S(2)}, u32[]{:S(2)}) collective-permute-start(bf16[256,512]{1,0:T(8,128)(2,1)} %get-tuple-element.224), channel_id=1, source_target_pairs={{0,1},{1,0},{2,3},{3,2},{4,5},{5,4},{6,7},{7,6},{8,9},{9,8},{10,11... | collective-permute-start | bytes 786440 | tf_op jit(solution)/shard_map/dhP/ppermute | solution.py:39
  63.1 8.7 %copy-start.3 = (bf16[1,1792,512]{2,1,0:T(8,128)(2,1)S(1)}, bf16[1,1792,512]{2,1,0:T(8,128)(2,1)}, u32[]{:S(2)}) copy-start(bf16[1,1792,512]{2,1,0:T(8,128)(2,1)} %param.27) | copy-start | bytes 5505028
  63.1 5.5 %copy-start.5 = (bf16[1792,512]{1,0:T(8,128)(2,1)S(1)}, bf16[1792,512]{1,0:T(8,128)(2,1)}, u32[]{:S(2)}) copy-start(bf16[1792,512]{1,0:T(8,128)(2,1)} %get-tuple-element.114.wd) | copy-start | bytes 5505028 | tf_op jit(solution)/shard_map/cond
  63.1 5.4 %copy-start.9 = (bf16[256,128]{1,0:T(8,128)(2,1)S(1)}, bf16[256,128]{1,0:T(8,128)(2,1)}, u32[]{:S(2)}) copy-start(bf16[256,128]{1,0:T(8,128)(2,1)} %get-tuple-element.117.gates) | copy-start | bytes 196612 | tf_op jit(solution)/shard_map/cond
  65.9 2.7 %collective-permute-start.8 = (bf16[256,1792]{1,0:T(8,128)(2,1)S(1)}, bf16[256,1792]{1,0:T(8,128)(2,1)S(1)}, u32[]{:S(2)}, u32[]{:S(2)}) collective-permute-start(bf16[256,1792]{1,0:T(8,128)(2,1)S(1)} %get-tuple-element.116.part), channel_id=1, source_target_pairs={{0,2},{2,0},{4,6},{6,4},{8,10},{10,8},{12,14},{14,12},{16,18},{18,... | collective-permute-start | bytes 2752520 | tf_op jit(solution)/shard_map/cond/branch_1_fun/eo/ppermute | solution.py:44
  70.2 16.4 %collective-permute-start.22 = (bf16[256,512]{1,0:T(8,128)(2,1)}, bf16[256,512]{1,0:T(8,128)(2,1)}, u32[]{:S(2)}, u32[]{:S(2)}) collective-permute-start(bf16[256,512]{1,0:T(8,128)(2,1)} %get-tuple-element.226), channel_id=1, source_target_pairs={{0,1},{1,0},{2,3},{3,2},{4,5},{5,4},{6,7},{7,6},{8,9},{9,8},{10,11... | collective-permute-start | bytes 786440 | tf_op jit(solution)/shard_map/dhN/ppermute | solution.py:39
  75.0 2.1 %collective-permute-start.9 = (bf16[128,1792]{1,0:T(8,128)(2,1)S(1)}, bf16[128,1792]{1,0:T(8,128)(2,1)S(1)}, u32[]{:S(2)}, u32[]{:S(2)}) collective-permute-start(bf16[128,1792]{1,0:T(8,128)(2,1)S(1)} %get-tuple-element.128), channel_id=1, source_target_pairs={{0,2},{2,0},{4,6},{6,4},{8,10},{10,8},{12,14},{14,12},{16,18},{18,... | collective-permute-start | bytes 1376264 | tf_op jit(solution)/shard_map/cond/branch_1_fun/dx/ppermute | solution.py:44
  81.3 1.8 %collective-permute-start.10 = (bf16[128,1792]{1,0:T(8,128)(2,1)S(1)}, bf16[128,1792]{1,0:T(8,128)(2,1)S(1)}, u32[]{:S(2)}, u32[]{:S(2)}) collective-permute-start(bf16[128,1792]{1,0:T(8,128)(2,1)S(1)} %get-tuple-element.139), channel_id=1, source_target_pairs={{0,2},{2,0},{4,6},{6,4},{8,10},{10,8},{12,14},{14,12},{16,18},{18,... | collective-permute-start | bytes 1376264 | tf_op jit(solution)/shard_map/cond/branch_1_fun/dx/ppermute | solution.py:44
  84.0 28.5 %collective-permute-start.23 = (bf16[64,1792]{1,0:T(8,128)(2,1)}, bf16[64,1792]{1,0:T(8,128)(2,1)S(1)}, u32[]{:S(2)}, u32[]{:S(2)}) collective-permute-start(bf16[64,1792]{1,0:T(8,128)(2,1)} %get-tuple-element.241), channel_id=1, source_target_pairs={{0,4},{1,5},{2,6},{3,7},{4,8},{5,9},{6,10},{7,11},{8,12},{9,13},{1... | collective-permute-start | bytes 688136 | tf_op jit(solution)/shard_map/rPs/ppermute | solution.py:34
  86.2 26.3 %collective-permute-start.25 = (bf16[64,1792]{1,0:T(8,128)(2,1)}, bf16[64,1792]{1,0:T(8,128)(2,1)S(1)}, u32[]{:S(2)}, u32[]{:S(2)}) collective-permute-start(bf16[64,1792]{1,0:T(8,128)(2,1)} %get-tuple-element.244), channel_id=1, source_target_pairs={{0,5},{1,4},{2,7},{3,6},{4,9},{5,8},{6,11},{7,10},{8,13},{9,12},{1... | collective-permute-start | bytes 688136 | tf_op jit(solution)/shard_map/rPo/ppermute | solution.py:34
  86.2 26.3 %collective-permute-start.26 = (bf16[64,1792]{1,0:T(8,128)(2,1)}, bf16[64,1792]{1,0:T(8,128)(2,1)S(1)}, u32[]{:S(2)}, u32[]{:S(2)}) collective-permute-start(bf16[64,1792]{1,0:T(8,128)(2,1)} %get-tuple-element.245), channel_id=1, source_target_pairs={{0,1},{1,0},{2,3},{3,2},{4,5},{5,4},{6,7},{7,6},{8,9},{9,8},{10,11... | collective-permute-start | bytes 688136 | tf_op jit(solution)/shard_map/rO/ppermute | solution.py:39
  86.6 16.0 %copy-start.6 = (bf16[256,512]{1,0:T(8,128)(2,1)S(1)}, bf16[256,512]{1,0:T(8,128)(2,1)}, u32[]{:S(2)}) copy-start(bf16[256,512]{1,0:T(8,128)(2,1)} %get-tuple-element.236.refs_9_) | copy-start | bytes 786436
  89.9 2.4 %collective-permute-start.11 = (bf16[128,1792]{1,0:T(8,128)(2,1)S(1)}, bf16[128,1792]{1,0:T(8,128)(2,1)S(1)}, u32[]{:S(2)}, u32[]{:S(2)}) collective-permute-start(bf16[128,1792]{1,0:T(8,128)(2,1)S(1)} %get-tuple-element.150), channel_id=1, source_target_pairs={{0,2},{2,0},{4,6},{6,4},{8,10},{10,8},{12,14},{14,12},{16,18},{18,... | collective-permute-start | bytes 1376264 | tf_op jit(solution)/shard_map/cond/branch_1_fun/dx/ppermute | solution.py:44
  93.2 19.3 %collective-permute-start.24 = (bf16[64,1792]{1,0:T(8,128)(2,1)}, bf16[64,1792]{1,0:T(8,128)(2,1)S(1)}, u32[]{:S(2)}, u32[]{:S(2)}) collective-permute-start(bf16[64,1792]{1,0:T(8,128)(2,1)} %get-tuple-element.243), channel_id=1, source_target_pairs={{0,252},{1,253},{2,254},{3,255},{4,0},{5,1},{6,2},{7,3},{8,4},{9,5... | collective-permute-start | bytes 688136 | tf_op jit(solution)/shard_map/rNs/ppermute | solution.py:34
  101.1 11.4 %collective-permute-start.27 = (bf16[64,1792]{1,0:T(8,128)(2,1)}, bf16[64,1792]{1,0:T(8,128)(2,1)S(1)}, u32[]{:S(2)}, u32[]{:S(2)}) collective-permute-start(bf16[64,1792]{1,0:T(8,128)(2,1)} %get-tuple-element.246), channel_id=1, source_target_pairs={{0,253},{1,252},{2,255},{3,254},{4,1},{5,0},{6,3},{7,2},{8,5},{9,4... | collective-permute-start | bytes 688136 | tf_op jit(solution)/shard_map/rNo/ppermute | solution.py:34
  102.6 10.0 %copy-start.7 = (bf16[64,1792]{1,0:T(8,128)(2,1)S(1)}, bf16[64,1792]{1,0:T(8,128)(2,1)}, u32[]{:S(2)}) copy-start(bf16[64,1792]{1,0:T(8,128)(2,1)} %get-tuple-element.242.s1) | copy-start | bytes 688132
